TPU v7x, 32 devices: a whole 2x2x4 slice. The times are simulated.
32 devices in a mesh: gx: 2 (over y), gy: 4 (over z), gz: 4 (over x, core).
Axes of the slice: x: 2, y: 2, z: 4, core: 2. Of those that a mesh axis runs over, the one named last changes fastest.
Arguments:
- solution: float32 [56, 9, 4096], P(None, None, ('gx', 'gy', 'gz')), may hold values from -6 to 6
- jacobians: float32 [3, 9, 9, 4096], P(None, None, None, ('gx', 'gy', 'gz')), may hold values from -2 to 2
- derivative_stiffness: float32 [3, 56, 56], replicated, may hold values from -0.75 to 0.75
- volume_stiffness: float32 [3, 56, 56], replicated, may hold values from -0.375 to 0.375
- face_project: float32 [4, 21, 56], replicated, may hold values from -0.75 to 0.75
- face_lift: float32 [4, 56, 21], replicated, may hold values from -0.625 to 0.625
- face_rotation: float32 [3, 21, 21], replicated, may hold values from -1.25 to 1.25
- local_solver: float32 [4, 9, 9, 4096], P(None, None, None, ('gx', 'gy', 'gz')), may hold values from -2 to 2
- neighbour_solver: float32 [4, 9, 9, 4096], P(None, None, None, ('gx', 'gy', 'gz')), may hold values from -2 to 2
- cluster: int32 [4096], P(('gx', 'gy', 'gz')), may hold values from 0 to 2
- neighbours: int32 [4, 4096], P(None, ('gx', 'gy', 'gz')), may hold values from 0 to 1279, as said below
- orient: int32 [4, 4096], P(None, ('gx', 'gy', 'gz')), may hold values from 0 to 2
- send_faces: int32 [6, 4096], P(None, ('gx', 'gy', 'gz')), may hold values from 0 to 511
- counts: int32 [6, 32], P(None, ('gx', 'gy', 'gz')), may hold values from 64 to 128, as said below
Outputs:
- advanced: float32 [56, 9, 4096], P(None, None, ('gx', 'gy', 'gz'))
Inputs may be any that keep to these rules, and one draw needn't show every extreme that they name: `neighbours`: below 512 a value names a face of the own partition; above, a slot of the blocks of one direction whose index is below the sending partition's count for that list. `send_faces`: each value is a local face j * 128 + n of the sending partition. `counts`: entry [k, p] is how many leading slots of partition p's list k are used; some entry equals 128.
All inputs are finite; a program needn't handle non-finite values.
Results may differ from a plain program's by a relative error of at most 0.0001.
Values sent between devices are 32-bit elements; how exact they have to be, the bound alone decides.
No kernel may reach another device: no remote copies, remote signals or barrier semaphores. Data moves between devices by JAX's collectives and lax.ppermute only.
A program may use at most 64 MiB of HBM per device.

v0:
```python
import functools
import math

import jax
import jax.numpy as jnp
from jax import lax
from jax.experimental import pallas as pl
from jax.experimental.pallas import tpu as pltpu
from jax.sharding import PartitionSpec as P

DERIVATIVES = 6
SUBSTEPS = 4
SPAN = 1.0
F32 = jnp.float32
BF16 = jnp.bfloat16
AXES = ("gx", "gy", "gz")


def rounded(size, unit):
    return -(-size // unit) * unit


def halves(value):
    high = value.astype(BF16)
    return high, (value - high.astype(F32)).astype(BF16)


def product(left, right):
    return jnp.dot(left, right, preferred_element_type=F32)


def exchange_plan(mesh):
    plan = []
    for number, axis in enumerate(AXES):
        size = mesh.shape[axis]
        if size == 1:
            continue
        if size == 2:
            plan.append((number, size, "pair0"))
        elif size % 2 == 0:
            plan.append((number, size, "pair0"))
            plan.append((number, size, "pair1"))
        else:
            plan.append((number, size, "up"))
            plan.append((number, size, "down"))
    return tuple(plan)


def partners(size, kind):
    if kind == "up":
        return [(i, (i + 1) % size) for i in range(size)]
    if kind == "down":
        return [(i, (i - 1) % size) for i in range(size)]
    first = 0 if kind == "pair0" else 1
    pairs = []
    for i in range(first, size + first, 2):
        low, high = i % size, (i + 1) % size
        pairs += [(low, high), (high, low)]
    return pairs


def lists_of(entry):
    number, size, kind = entry
    place = lax.axis_index(AXES[number])
    if kind == "up":
        return 2 * number, 2 * number, place > 0
    if kind == "down":
        return 2 * number + 1, 2 * number + 1, place < size - 1
    parity = lax.rem(place, 2)
    upper = parity if kind == "pair0" else 1 - parity
    exists = jnp.where(upper == 1, place > 0, place < size - 1)
    return 2 * number + upper, 2 * number + 1 - upper, exists


class Sizes:
    def __init__(self, solution, face_project, send_faces, plan):
        self.basis, self.quantities, self.elements = solution.shape
        self.faces, self.face_basis, _ = face_project.shape
        self.slots = send_faces.shape[1]
        self.plan = plan
        self.padded = rounded(self.basis, 16)
        self.face_rows = rounded(self.face_basis, 8)
        self.block = self.quantities * self.face_rows
        self.block_padded = rounded(self.block, 16)
        self.columns = self.quantities * self.elements
        self.face_total = self.faces * self.elements
        self.lifted = self.faces * self.face_rows
        self.rotations = 3

    def groups(self):
        return [(k, min(16, self.basis - k)) for k in range(0, self.basis, 16)]


def left_parts(scratch, pieces, width):
    scratch[...] = jnp.zeros_like(scratch)
    for row, column, value in pieces:
        high = value.astype(BF16).astype(F32)
        rows, columns = value.shape
        scratch[row : row + rows, column : column + columns] = high
        scratch[row : row + rows, width + column : width + column + columns] = high
        scratch[row : row + rows, 2 * width + column : 2 * width + column + columns] = value - high
    return scratch[...].astype(BF16)


def one_hot(shape, targets, offset):
    rows = lax.broadcasted_iota(jnp.int32, shape, 0)
    return jnp.where(rows == targets - offset, 1.0, 0.0).astype(BF16)


def period_of(cluster):
    return jnp.left_shift(jnp.ones_like(cluster), cluster)


def weights_of(cluster, substep):
    offset = (substep & (period_of(cluster) - 1)).astype(F32)
    step = SPAN / SUBSTEPS
    upper, lower = (offset + 1.0) * step, offset * step
    rows, high, low = [], upper, lower
    for power in range(DERIVATIVES):
        rows.append((high - low) * (1.0 / math.factorial(power + 1)))
        high, low = high * upper, low * lower
    return rows


def put_halves(target, width, row, column, value):
    high, low = halves(value)
    rows, columns = value.shape
    target[row : row + rows, column : column + columns] = high
    target[width + row : width + row + rows, column : column + columns] = low
    target[2 * width + row : 2 * width + row + rows, column : column + columns] = high


def contract(z, mixed, jacobians, first, rows):
    totals = [None] * z.quantities
    for d in range(3):
        for q in range(z.quantities):
            start = d * z.basis + first
            value = mixed[start : start + rows, q * z.elements : (q + 1) * z.elements]
            for p in range(z.quantities):
                term = value * jacobians[q, p, d : d + 1, :]
                totals[p] = term if totals[p] is None else totals[p] + term
    return totals


def full_rows(value, rows):
    short = rows - value.shape[0]
    if short == 0:
        return value
    return jnp.concatenate([value, jnp.zeros((short, value.shape[1]), value.dtype)], axis=0)


def predict(z, substep, cluster, state, jacobians, stiff, project, send_hot, outgoing, table, faces, moments, rhs, mixed, total, weights):
    e = z.elements
    for power, row in enumerate(weights_of(cluster[...], substep)):
        weights[power] = jnp.broadcast_to(row, (8, e))
    for q in range(z.quantities):
        for first, rows in z.groups():
            value = state(q, first, rows)
            total[q, first : first + rows, :] = value * weights[0, 0:1, :]
            put_halves(rhs, z.padded, first, q * e, full_rows(value, 16))

    def derivative(power, carry):
        mixed[...] = product(stiff[...], rhs[...])
        weight = weights[power]
        for first, rows in z.groups():
            sums = contract(z, mixed, jacobians, first, rows)
            for p in range(z.quantities):
                total[p, first : first + rows, :] += sums[p] * weight[0:1, :]
                put_halves(rhs, z.padded, first, p * e, full_rows(sums[p], 16))
        return carry

    lax.fori_loop(1, DERIVATIVES, derivative, 0)
    for q in range(z.quantities):
        for first, rows in z.groups():
            put_halves(moments, z.padded, first, q * e, full_rows(total[q, first : first + rows, :], 16))
    projected = product(project[...], moments[...])
    faces[...] = projected
    r = z.face_rows
    for j in range(z.faces):
        pieces = [projected[j * r : (j + 1) * r, q * e : (q + 1) * e] for q in range(z.quantities)]
        high, low = halves(full_rows(jnp.concatenate(pieces, axis=0), z.block_padded))
        table[: z.block_padded, j * e : (j + 1) * e] = high
        table[z.block_padded :, j * e : (j + 1) * e] = low
    picked = product(table[...], send_hot[...])
    for t, target in enumerate(outgoing):
        columns = slice(t * z.slots, (t + 1) * z.slots)
        target[...] = picked[: z.block, columns] + picked[z.block_padded : z.block_padded + z.block, columns]


def first_kernel(z, *refs):
    count = len(z.plan)
    solution, jacobians, stiffness, projection, cluster, send_faces, counts = refs[:7]
    outgoing = refs[7 : 7 + count]
    table, faces, moments, stiff, project, send_hot = refs[7 + count : 13 + count]
    rhs, mixed, total, weights, wide_stiff, wide_project = refs[13 + count :]
    b = z.basis
    stiff[...] = left_parts(wide_stiff, [(d * b, 0, -stiffness[d]) for d in range(3)], z.padded)
    project[...] = left_parts(
        wide_project, [(j * z.face_rows, 0, projection[:, j, :]) for j in range(z.faces)], z.padded
    )
    slot = lax.broadcasted_iota(jnp.int32, (1, z.slots), 1)
    for t, entry in enumerate(z.plan):
        chosen = lists_of(entry)[0]
        wanted = jnp.where(slot < counts[0, chosen], send_faces[pl.ds(chosen, 1), :], -1)
        send_hot[:, t * z.slots : (t + 1) * z.slots] = one_hot((z.face_total, z.slots), wanted, 0)
    predict(
        z, 0, cluster, lambda q, k, n: solution[q, k : k + n, :], jacobians, stiff, project, send_hot,
        outgoing, table, faces, moments, rhs, mixed, total, weights,
    )


def tables_kernel(z, *refs):
    volume, lift, rotation, neighbours, orient = refs[:5]
    volume_left, lift_left, turned_left, picks, own_hot, far_hot = refs[5:11]
    wide_volume, wide_lift, wide_turned = refs[11:]
    e, r, f = z.elements, z.face_rows, z.face_basis
    volume_left[...] = left_parts(wide_volume, [(d * z.basis, 0, volume[d]) for d in range(3)], z.padded)
    plain, turned = [], []
    for i in range(z.faces):
        face = jnp.transpose(lift[:, i, :], (1, 0))
        plain.append((0, i * r, face))
        for o in range(z.rotations):
            value = jnp.dot(face, rotation[o], precision=lax.Precision.HIGHEST, preferred_element_type=F32)
            turned.append((0, o * z.lifted + i * r, value))
    lift_left[...] = left_parts(wide_lift, plain, z.lifted)
    turned_left[...] = left_parts(wide_turned, turned, z.rotations * z.lifted)
    for o in range(z.rotations):
        rows = [
            jnp.broadcast_to(jnp.where(orient[i : i + 1, :] == o, 1.0, 0.0), (r, e)) for i in range(z.faces)
        ]
        picks[o] = jnp.concatenate(rows, axis=0).astype(BF16)
    for i in range(z.faces):
        wanted = neighbours[i : i + 1, :]
        own_hot[:, i * e : (i + 1) * e] = one_hot((z.face_total, e), wanted, 0)
        for t, entry in enumerate(z.plan):
            _, direction, exists = lists_of(entry)
            offset = jnp.where(exists, z.face_total + direction * z.slots, -z.slots)
            far_hot[t * z.slots : (t + 1) * z.slots, i * e : (i + 1) * e] = one_hot((z.slots, e), wanted, offset)


def inner_kernel(z, running, table, faces, moments, jacobians, local_solver, volume_left, lift_left, own_hot, gathered, partial, mixed, rhs):
    e, r = z.elements, z.face_rows
    picked = product(table[...], own_hot[...])
    gathered[...] = picked[: z.block, :] + picked[z.block_padded : z.block_padded + z.block, :]
    for i in range(z.faces):
        sums = [None] * z.quantities
        for q in range(z.quantities):
            value = faces[i * r : (i + 1) * r, q * e : (q + 1) * e]
            for p in range(z.quantities):
                term = value * local_solver[q, p, i : i + 1, :]
                sums[p] = term if sums[p] is None else sums[p] + term
        for p in range(z.quantities):
            partial_rows = slice(i * r, (i + 1) * r)
            mixed[partial_rows, p * e : (p + 1) * e] = sums[p]
    put_halves(rhs, z.lifted, 0, 0, mixed[: z.lifted, :])
    lifted = product(lift_left[...], rhs[...])
    for q in range(z.quantities):
        partial[q] = running[q] - lifted[:, q * e : (q + 1) * e]
    mixed[...] = product(volume_left[...], moments[...])
    for first, rows in z.groups():
        sums = contract(z, mixed, jacobians, first, rows)
        for p in range(z.quantities):
            partial[p, first : first + rows, :] += sums[p]


def neighbour_flux(z, incoming, gathered, neighbour_solver, picks, far_hot, turned_left, received, blocks, turned):
    e, r, b = z.elements, z.face_rows, z.block
    for t, source in enumerate(incoming):
        high, low = halves(full_rows(source[...], z.block_padded))
        received[: z.block_padded, t * z.slots : (t + 1) * z.slots] = high
        received[z.block_padded :, t * z.slots : (t + 1) * z.slots] = low
    picked = product(received[...], far_hot[...])
    blocks[...] = gathered[...] + picked[:b, :] + picked[z.block_padded : z.block_padded + b, :]
    width = z.rotations * z.lifted
    for i in range(0, z.faces, 2):
        per_face = []
        for j in (i, i + 1):
            sums = [None] * z.quantities
            for q in range(z.quantities):
                value = blocks[q * r : (q + 1) * r, j * e : (j + 1) * e]
                for p in range(z.quantities):
                    term = value * neighbour_solver[q, p, j : j + 1, :]
                    sums[p] = term if sums[p] is None else sums[p] + term
            per_face.append(sums)
        for p in range(z.quantities):
            high, low = halves(jnp.concatenate([per_face[0][p], per_face[1][p]], axis=0))
            for o in range(z.rotations):
                pick = picks[o, i * r : (i + 2) * r, :]
                row = o * z.lifted + i * r
                chosen = high * pick
                turned[row : row + 2 * r, p * e : (p + 1) * e] = chosen
                turned[2 * width + row : 2 * width + row + 2 * r, p * e : (p + 1) * e] = chosen
                turned[width + row : width + row + 2 * r, p * e : (p + 1) * e] = low * pick
    return product(turned_left[...], turned[...])


def outer_kernel(z, substep, *refs):
    count = len(z.plan)
    incoming = refs[:count]
    (gathered, partial, solution, neighbour_solver, picks, far_hot, turned_left, jacobians, stiff, project, send_hot, cluster) = refs[
        count : count + 12
    ]
    outgoing = refs[count + 12 : 2 * count + 12]
    table, faces, moments, updated, running = refs[2 * count + 12 : 2 * count + 17]
    rhs, mixed, total, weights, received, blocks, turned = refs[2 * count + 17 :]
    e = z.elements
    flux = neighbour_flux(
        z, incoming, gathered, neighbour_solver, picks, far_hot, turned_left, received, blocks, turned
    )
    ending = ((substep + 1) & (period_of(cluster[...]) - 1)) == 0
    for q in range(z.quantities):
        value = partial[q] - flux[:, q * e : (q + 1) * e]
        running[q] = value
        updated[q] = jnp.where(ending, value, solution[q])
    predict(
        z, substep + 1, cluster, lambda q, k, n: updated[q, k : k + n, :], jacobians, stiff, project, send_hot,
        outgoing, table, faces, moments, rhs, mixed, total, weights,
    )


def last_kernel(z, *refs):
    count = len(z.plan)
    incoming = refs[:count]
    gathered, partial, neighbour_solver, picks, far_hot, turned_left = refs[count : count + 6]
    advanced = refs[count + 6]
    received, blocks, turned = refs[count + 7 :]
    e = z.elements
    flux = neighbour_flux(
        z, incoming, gathered, neighbour_solver, picks, far_hot, turned_left, received, blocks, turned
    )
    for q in range(z.quantities):
        advanced[q] = partial[q] - flux[:, q * e : (q + 1) * e]


def call(body, outs, scratch, cost, arguments, scalars=()):
    in_specs = [
        pl.BlockSpec(memory_space=pltpu.SMEM if n in scalars else pltpu.VMEM) for n in range(len(arguments))
    ]
    return pl.pallas_call(
        body,
        out_shape=[jax.ShapeDtypeStruct(shape, kind) for shape, kind in outs],
        in_specs=in_specs,
        out_specs=[pl.BlockSpec(memory_space=pltpu.VMEM)] * len(outs),
        scratch_shapes=[pltpu.VMEM(shape, kind) for shape, kind in scratch],
        cost_estimate=pl.CostEstimate(flops=cost, bytes_accessed=1 << 20, transcendentals=0),
        compiler_params=pltpu.CompilerParams(vmem_limit_bytes=24 << 20),
    )(*arguments)


def local(
    plan,
    solution,
    jacobians,
    derivative_stiffness,
    volume_stiffness,
    face_project,
    face_lift,
    face_rotation,
    local_solver,
    neighbour_solver,
    cluster,
    neighbours,
    orient,
    send_faces,
    counts,
):
    z = Sizes(solution, face_project, send_faces, plan)
    count = len(plan)
    state = solution.transpose(1, 0, 2)
    jacobians = jacobians.transpose(1, 2, 0, 3)
    local_solver = local_solver.transpose(1, 2, 0, 3)
    neighbour_solver = neighbour_solver.transpose(1, 2, 0, 3)
    projection = face_project.transpose(1, 0, 2)
    lift = face_lift.transpose(2, 0, 1)
    cluster = cluster.reshape(1, -1)
    counts = counts.reshape(1, -1)

    block = ((z.block, z.slots), F32)
    table = ((2 * z.block_padded, z.face_total), BF16)
    faces = ((z.lifted, z.columns), F32)
    moments = ((3 * z.padded, z.columns), BF16)
    stiff = ((3 * z.basis, 3 * z.padded), BF16)
    project = ((z.lifted, 3 * z.padded), BF16)
    field = ((z.quantities, z.basis, z.elements), F32)
    gathered = ((z.block, z.face_total), F32)
    send_hot = ((z.face_total, count * z.slots), BF16)
    far_hot = ((count * z.slots, z.face_total), BF16)
    own_hot = ((z.face_total, z.face_total), BF16)
    lift_left = ((z.basis, 3 * z.lifted), BF16)
    turned_left = ((z.basis, 3 * z.rotations * z.lifted), BF16)
    picks = ((z.rotations, z.lifted, z.elements), BF16)
    mixed = ((3 * z.basis, z.columns), F32)
    weights = ((DERIVATIVES, 8, z.elements), F32)
    received = ((2 * z.block_padded, count * z.slots), BF16)
    turned = ((3 * z.rotations * z.lifted, z.columns), BF16)

    def wide(entry):
        return (entry[0], F32)

    def trade(outgoing):
        return [
            lax.ppermute(value, AXES[number], partners(size, kind))
            for value, (number, size, kind) in zip(outgoing, plan)
        ]

    results = call(
        functools.partial(first_kernel, z),
        [block] * count + [table, faces, moments, stiff, project, send_hot],
        [moments, mixed, field, weights, wide(stiff), wide(project)],
        10_000_000,
        (state, jacobians, derivative_stiffness, projection, cluster, send_faces, counts),
        scalars=(6,),
    )
    outgoing = results[:count]
    table_now, faces_now, moments_now, stiff_left, project_left, send_matrix = results[count:]
    running = state
    for substep in range(SUBSTEPS):
        incoming = trade(outgoing)
        if substep == 0:
            volume_left, lift_plain, lift_turned, orient_picks, own_matrix, far_matrix = call(
                functools.partial(tables_kernel, z),
                [stiff, lift_left, turned_left, picks, own_hot, far_hot],
                [wide(stiff), wide(lift_left), wide(turned_left)],
                1_000_000,
                (volume_stiffness, lift, face_rotation, neighbours, orient),
            )
        gathered_now, partial = call(
            functools.partial(inner_kernel, z),
            [gathered, field],
            [mixed, ((3 * z.lifted, z.columns), BF16)],
            10_000_000,
            (running, table_now, faces_now, moments_now, jacobians, local_solver, volume_left, lift_plain, own_matrix),
        )
        if substep == SUBSTEPS - 1:
            (advanced,) = call(
                functools.partial(last_kernel, z),
                [field],
                [received, gathered, turned],
                10_000_000,
                (*incoming, gathered_now, partial, neighbour_solver, orient_picks, far_matrix, lift_turned),
            )
            return advanced.transpose(1, 0, 2)
        results = call(
            functools.partial(outer_kernel, z, substep),
            [block] * count + [table, faces, moments, field, field],
            [moments, mixed, field, weights, received, gathered, turned],
            10_000_000,
            (
                *incoming, gathered_now, partial, state, neighbour_solver, orient_picks, far_matrix, lift_turned,
                jacobians, stiff_left, project_left, send_matrix, cluster,
            ),
        )
        outgoing = results[:count]
        table_now, faces_now, moments_now, state, running = results[count:]


def solution(mesh):
    spread = ("gx", "gy", "gz")
    return jax.shard_map(
        functools.partial(local, exchange_plan(mesh)),
        mesh=mesh,
        in_specs=(
            P(None, None, spread),
            P(None, None, None, spread),
            P(),
            P(),
            P(),
            P(),
            P(),
            P(None, None, None, spread),
            P(None, None, None, spread),
            P(spread),
            P(None, spread),
            P(None, spread),
            P(None, spread),
            P(None, spread),
        ),
        out_specs=P(None, None, spread),
        check_vma=False,
    )
```

profile of v0, /device:TPU:0, one launch (start us, length us, event | category | flops | bytes accessed | tf_op | source)
XLA Modules:
  0.0 71.0 jit_solution(4169273457343966049)
XLA Ops:
  0.0 0.7 copy-done.12
  0.7 0.0 copy-done.11
  0.7 0.0 copy-done.15
  0.7 0.9 %copy-done = f32[3,9,9,128]{3,0,2,1:T(4,128)S(1)} copy-done((f32[3,9,9,128]{3,0,2,1:T(4,128)S(1)}, f32[3,9,9,128]{3,0,2,1:T(4,128)}, u32[]{:S(2)}) %copy-start) | copy-done | bytes 124440
  1.6 0.9 %copy-done.4 = f32[56,9,128]{2,0,1:T(8,128)S(1)} copy-done((f32[56,9,128]{2,0,1:T(8,128)S(1)}, f32[56,9,128]{2,0,1:T(8,128)}, u32[]{:S(2)}) %copy-start.4) | copy-done | bytes 258072
  2.6 0.9 %copy-done.7 = f32[3,56,56]{2,1,0:T(8,128)S(1)} copy-done((f32[3,56,56]{2,1,0:T(8,128)S(1)}, f32[3,56,56]{2,1,0:T(8,128)}, u32[]{:S(2)}) %copy-start.7) | copy-done | bytes 37656
  3.5 0.8 %copy-done.9 = f32[4,21,56]{2,0,1:T(4,128)S(1)} copy-done((f32[4,21,56]{2,0,1:T(4,128)S(1)}, f32[4,21,56]{2,0,1:T(4,128)}, u32[]{:S(2)}) %copy-start.9) | copy-done | bytes 18840
  4.2 0.0 copy-start.3
  4.3 6.0 %shard_map.136 = (f32[216,128]{1,0:T(8,128)S(1)}, f32[216,128]{1,0:T(8,128)S(1)}, f32[216,128]{1,0:T(8,128)S(1)}, f32[216,128]{1,0:T(8,128)S(1)}, f32[216,128]{1...) custom-call(f32[9,56,128]{2,1,0:T(8,128)S(1)} %bitcast.25, ...), custom_call_target="tpu_custom_call" | custom-call | flops 10000000 | bytes 1048576 | tf_op jit(solution)/shard_map/pallas_call | solution.py:339
  10.3 0.0 copy-start.1
  10.3 3.1 %collective-permute-start = (f32[216,128]{1,0:T(8,128)S(1)}, f32[216,128]{1,0:T(8,128)S(1)}, u32[]{:S(2)}, u32[]{:S(2)}) collective-permute-start(f32[216,128]{1,0:T(8,128)S(1)} %get-tuple-element.59), channel_id=1, source_target_pairs={{0,16},{16,0},{1,17},{17,1},{2,18},{18,2},{3,19},{19,3},{4,20},{20... | collective-permute-start | bytes 331784 | tf_op jit(solution)/shard_map/ppermute | solution.py:402
  13.3 1.6 %collective-permute-start.1 = (f32[216,128]{1,0:T(8,128)S(1)}, f32[216,128]{1,0:T(8,128)S(1)}, u32[]{:S(2)}, u32[]{:S(2)}) collective-permute-start(f32[216,128]{1,0:T(8,128)S(1)} %get-tuple-element.60), channel_id=1, source_target_pairs={{0,4},{4,0},{8,12},{12,8},{1,5},{5,1},{9,13},{13,9},{2,6},{6,2},{1... | collective-permute-start | bytes 331784 | tf_op jit(solution)/shard_map/ppermute | solution.py:402
  14.9 2.5 %collective-permute-start.2 = (f32[216,128]{1,0:T(8,128)S(1)}, f32[216,128]{1,0:T(8,128)S(1)}, u32[]{:S(2)}, u32[]{:S(2)}) collective-permute-start(f32[216,128]{1,0:T(8,128)S(1)} %get-tuple-element.61), channel_id=1, source_target_pairs={{4,8},{8,4},{12,0},{0,12},{5,9},{9,5},{13,1},{1,13},{6,10},{10,6},... | collective-permute-start | bytes 331784 | tf_op jit(solution)/shard_map/ppermute | solution.py:402
  17.4 0.0 collective-permute-start.3
  17.4 1.6 %collective-permute-start.4 = (f32[216,128]{1,0:T(8,128)S(1)}, f32[216,128]{1,0:T(8,128)S(1)}, u32[]{:S(2)}, u32[]{:S(2)}) collective-permute-start(f32[216,128]{1,0:T(8,128)S(1)} %get-tuple-element.63), channel_id=1, source_target_pairs={{1,2},{2,1},{3,0},{0,3},{5,6},{6,5},{7,4},{4,7},{9,10},{10,9},{11,... | collective-permute-start | bytes 331784 | tf_op jit(solution)/shard_map/ppermute | solution.py:402
  19.0 0.0 copy-done.14
  19.0 0.0 copy-start.10
  19.0 0.8 %copy-done.10 = f32[3,21,21]{2,1,0:T(8,128)S(1)} copy-done((f32[3,21,21]{2,1,0:T(8,128)S(1)}, f32[3,21,21]{2,1,0:T(8,128)}, u32[]{:S(2)}) %copy-start.10) | copy-done | bytes 5316
  19.8 1.2 %shard_map.137 = (bf16[168,192]{1,0:T(8,128)(2,1)S(1)}, bf16[56,288]{1,0:T(8,128)(2,1)S(1)}, bf16[56,864]{1,0:T(8,128)(2,1)S(1)}, bf16[3,96,128]{2,1,0:T(8,128)(...) custom-call(f32[3,56,56]{2,1,0:T(8,128)S(1)} %copy-done.6, f32[21,4,56]{2,1,0:T(4,128)S(1)} %bitcast.28, ...), custom_call_target="tpu_custom_call" | custom-call | flops 1000000 | bytes 1048576 | tf_op jit(solution)/shard_map/pallas_call | solution.py:339
  21.0 0.0 copy-start.2
  21.0 1.3 %shard_map.138 = (f32[216,512]{1,0:T(8,128)S(1)}, f32[9,56,128]{2,1,0:T(8,128)S(1)}) custom-call(f32[9,56,128]{2,1,0:T(8,128)S(1)} %bitcast.26, bf16[448,512]{1,0:T(8,128)(2,1)S(1)} %get-tuple-element.64.table, f32[96,1152]{1,0:T(8,128)S(1)} %get-tuple-element.65.faces, bf16[192,1152]{1,0:T(8,128)(2,1)S(1)} %get-tuple-element.66.moments, ...), custom_call_target="tpu_custom_call" | custom-call | flops 10000000 | bytes 1048576 | tf_op jit(solution)/shard_map/pallas_call | solution.py:339
  22.3 0.0 collective-permute-done.refs_0_
  22.3 0.0 collective-permute-done.1.refs_1_
  22.3 0.0 collective-permute-done.2.refs_2_
  22.4 0.0 collective-permute-done.3.refs_3_
  22.4 0.0 collective-permute-done.4.refs_4_
  22.4 0.0 copy-done.2
  22.4 6.4 %shard_map.139 = (f32[216,128]{1,0:T(8,128)S(1)}, f32[216,128]{1,0:T(8,128)S(1)}, f32[216,128]{1,0:T(8,128)S(1)}, f32[216,128]{1,0:T(8,128)S(1)}, f32[216,128]{1...) custom-call(f32[216,128]{1,0:T(8,128)S(1)} %collective-permute-done., ...), custom_call_target="tpu_custom_call" | custom-call | flops 10000000 | bytes 1048576 | tf_op jit(solution)/shard_map/pallas_call | solution.py:339
  28.8 0.6 collective-permute-start.5
  29.4 0.7 collective-permute-start.6
  30.1 2.5 %collective-permute-start.7 = (f32[216,128]{1,0:T(8,128)S(1)}, f32[216,128]{1,0:T(8,128)S(1)}, u32[]{:S(2)}, u32[]{:S(2)}) collective-permute-start(f32[216,128]{1,0:T(8,128)S(1)} %get-tuple-element.80), channel_id=1, source_target_pairs={{4,8},{8,4},{12,0},{0,12},{5,9},{9,5},{13,1},{1,13},{6,10},{10,6},... | collective-permute-start | bytes 331784 | tf_op jit(solution)/shard_map/ppermute | solution.py:402
  32.6 0.0 collective-permute-start.8
  32.6 1.6 %collective-permute-start.9 = (f32[216,128]{1,0:T(8,128)S(1)}, f32[216,128]{1,0:T(8,128)S(1)}, u32[]{:S(2)}, u32[]{:S(2)}) collective-permute-start(f32[216,128]{1,0:T(8,128)S(1)} %get-tuple-element.82), channel_id=1, source_target_pairs={{1,2},{2,1},{3,0},{0,3},{5,6},{6,5},{7,4},{4,7},{9,10},{10,9},{11,... | collective-permute-start | bytes 331784 | tf_op jit(solution)/shard_map/ppermute | solution.py:402
  34.2 1.3 %shard_map.140 = (f32[216,512]{1,0:T(8,128)S(1)}, f32[9,56,128]{2,1,0:T(8,128)S(1)}) custom-call(f32[9,56,128]{2,1,0:T(8,128)S(1)} %get-tuple-element.83.running, bf16[448,512]{1,0:T(8,128)(2,1)S(1)} %get-tuple-element.84.table, f32[96,1152]{1,0:T(8,128)S(1)} %get-tuple-element.85.faces, bf16[192,1152]{1,0:T(8,128)(2,1)S(1)} %get-tuple-element.86.moments, ...), custom_call_target="tpu_custom_call" | custom-call | flops 10000000 | bytes 1048576 | tf_op jit(solution)/shard_map/pallas_call | solution.py:339
  35.5 0.0 collective-permute-done.5.refs_0_
  35.5 0.0 collective-permute-done.6.refs_1_
  35.5 2.1 %collective-permute-done.7.refs_2_ = f32[216,128]{1,0:T(8,128)S(1)} collective-permute-done((f32[216,128]{1,0:T(8,128)S(1)}, f32[216,128]{1,0:T(8,128)S(1)}, u32[]{:S(2)}, u32[]{:S(2)}) %collective-permute-start.7) | collective-permute-done | bytes 110624 | tf_op jit(solution)/shard_map/ppermute | solution.py:402
  37.6 0.0 collective-permute-done.8.refs_3_
  37.6 0.0 collective-permute-done.9.refs_4_
  37.6 6.6 %shard_map.141 = (f32[216,128]{1,0:T(8,128)S(1)}, f32[216,128]{1,0:T(8,128)S(1)}, f32[216,128]{1,0:T(8,128)S(1)}, f32[216,128]{1,0:T(8,128)S(1)}, f32[216,128]{1...) custom-call(f32[216,128]{1,0:T(8,128)S(1)} %collective-permute-done., ...), custom_call_target="tpu_custom_call" | custom-call | flops 10000000 | bytes 1048576 | tf_op jit(solution)/shard_map/pallas_call | solution.py:339
  44.3 1.6 %collective-permute-start.10 = (f32[216,128]{1,0:T(8,128)S(1)}, f32[216,128]{1,0:T(8,128)S(1)}, u32[]{:S(2)}, u32[]{:S(2)}) collective-permute-start(f32[216,128]{1,0:T(8,128)S(1)} %get-tuple-element.90), channel_id=1, source_target_pairs={{0,16},{16,0},{1,17},{17,1},{2,18},{18,2},{3,19},{19,3},{4,20},{20... | collective-permute-start | bytes 331784 | tf_op jit(solution)/shard_map/ppermute | solution.py:402
  45.9 0.7 %collective-permute-start.11 = (f32[216,128]{1,0:T(8,128)S(1)}, f32[216,128]{1,0:T(8,128)S(1)}, u32[]{:S(2)}, u32[]{:S(2)}) collective-permute-start(f32[216,128]{1,0:T(8,128)S(1)} %get-tuple-element.91), channel_id=1, source_target_pairs={{0,4},{4,0},{8,12},{12,8},{1,5},{5,1},{9,13},{13,9},{2,6},{6,2},{1... | collective-permute-start | bytes 331784 | tf_op jit(solution)/shard_map/ppermute | solution.py:402
  46.6 1.7 %collective-permute-start.12 = (f32[216,128]{1,0:T(8,128)S(1)}, f32[216,128]{1,0:T(8,128)S(1)}, u32[]{:S(2)}, u32[]{:S(2)}) collective-permute-start(f32[216,128]{1,0:T(8,128)S(1)} %get-tuple-element.92), channel_id=1, source_target_pairs={{4,8},{8,4},{12,0},{0,12},{5,9},{9,5},{13,1},{1,13},{6,10},{10,6},... | collective-permute-start | bytes 331784 | tf_op jit(solution)/shard_map/ppermute | solution.py:402
  48.2 0.0 collective-permute-start.13
  48.2 1.6 %collective-permute-start.14 = (f32[216,128]{1,0:T(8,128)S(1)}, f32[216,128]{1,0:T(8,128)S(1)}, u32[]{:S(2)}, u32[]{:S(2)}) collective-permute-start(f32[216,128]{1,0:T(8,128)S(1)} %get-tuple-element.94), channel_id=1, source_target_pairs={{1,2},{2,1},{3,0},{0,3},{5,6},{6,5},{7,4},{4,7},{9,10},{10,9},{11,... | collective-permute-start | bytes 331784 | tf_op jit(solution)/shard_map/ppermute | solution.py:402
  49.9 1.3 %shard_map.142 = (f32[216,512]{1,0:T(8,128)S(1)}, f32[9,56,128]{2,1,0:T(8,128)S(1)}) custom-call(f32[9,56,128]{2,1,0:T(8,128)S(1)} %get-tuple-element.95.running, bf16[448,512]{1,0:T(8,128)(2,1)S(1)} %get-tuple-element.96.table, f32[96,1152]{1,0:T(8,128)S(1)} %get-tuple-element.97.faces, bf16[192,1152]{1,0:T(8,128)(2,1)S(1)} %get-tuple-element.98.moments, ...), custom_call_target="tpu_custom_call" | custom-call | flops 10000000 | bytes 1048576 | tf_op jit(solution)/shard_map/pallas_call | solution.py:339
  51.1 0.0 collective-permute-done.10.refs_0_
  51.2 0.1 collective-permute-done.11.refs_1_
  51.2 2.2 %collective-permute-done.12.refs_2_ = f32[216,128]{1,0:T(8,128)S(1)} collective-permute-done((f32[216,128]{1,0:T(8,128)S(1)}, f32[216,128]{1,0:T(8,128)S(1)}, u32[]{:S(2)}, u32[]{:S(2)}) %collective-permute-start.12) | collective-permute-done | bytes 110624 | tf_op jit(solution)/shard_map/ppermute | solution.py:402
  53.4 0.0 collective-permute-done.13.refs_3_
  53.4 0.0 collective-permute-done.14.refs_4_
  53.4 6.8 %shard_map.143 = (f32[216,128]{1,0:T(8,128)S(1)}, f32[216,128]{1,0:T(8,128)S(1)}, f32[216,128]{1,0:T(8,128)S(1)}, f32[216,128]{1,0:T(8,128)S(1)}, f32[216,128]{1...) custom-call(f32[216,128]{1,0:T(8,128)S(1)} %collective-permute-done., ...), custom_call_target="tpu_custom_call" | custom-call | flops 10000000 | bytes 1048576 | tf_op jit(solution)/shard_map/pallas_call | solution.py:339
  60.2 0.5 collective-permute-start.15
  60.7 1.3 %collective-permute-start.16 = (f32[216,128]{1,0:T(8,128)S(1)}, f32[216,128]{1,0:T(8,128)S(1)}, u32[]{:S(2)}, u32[]{:S(2)}) collective-permute-start(f32[216,128]{1,0:T(8,128)S(1)} %get-tuple-element.103), channel_id=1, source_target_pairs={{0,4},{4,0},{8,12},{12,8},{1,5},{5,1},{9,13},{13,9},{2,6},{6,2},{1... | collective-permute-start | bytes 331784 | tf_op jit(solution)/shard_map/ppermute | solution.py:402
  62.1 1.5 %collective-permute-start.17 = (f32[216,128]{1,0:T(8,128)S(1)}, f32[216,128]{1,0:T(8,128)S(1)}, u32[]{:S(2)}, u32[]{:S(2)}) collective-permute-start(f32[216,128]{1,0:T(8,128)S(1)} %get-tuple-element.104), channel_id=1, source_target_pairs={{4,8},{8,4},{12,0},{0,12},{5,9},{9,5},{13,1},{1,13},{6,10},{10,6},... | collective-permute-start | bytes 331784 | tf_op jit(solution)/shard_map/ppermute | solution.py:402
  63.6 0.0 collective-permute-start.18
  63.6 1.6 %collective-permute-start.19 = (f32[216,128]{1,0:T(8,128)S(1)}, f32[216,128]{1,0:T(8,128)S(1)}, u32[]{:S(2)}, u32[]{:S(2)}) collective-permute-start(f32[216,128]{1,0:T(8,128)S(1)} %get-tuple-element.106), channel_id=1, source_target_pairs={{1,2},{2,1},{3,0},{0,3},{5,6},{6,5},{7,4},{4,7},{9,10},{10,9},{11,... | collective-permute-start | bytes 331784 | tf_op jit(solution)/shard_map/ppermute | solution.py:402
  65.1 1.3 %shard_map.144 = (f32[216,512]{1,0:T(8,128)S(1)}, f32[9,56,128]{2,1,0:T(8,128)S(1)}) custom-call(f32[9,56,128]{2,1,0:T(8,128)S(1)} %get-tuple-element.107.running, bf16[448,512]{1,0:T(8,128)(2,1)S(1)} %get-tuple-element.108.table, f32[96,1152]{1,0:T(8,128)S(1)} %get-tuple-element.109.faces, bf16[192,1152]{1,0:T(8,128)(2,1)S(1)} %get-tuple-element.110.moments, ...), custom_call_target="tpu_custom_call" | custom-call | flops 10000000 | bytes 1048576 | tf_op jit(solution)/shard_map/pallas_call | solution.py:339
  66.4 0.0 collective-permute-done.15.refs_0_
  66.4 0.0 collective-permute-done.16.refs_1_
  66.4 2.3 %collective-permute-done.17.refs_2_ = f32[216,128]{1,0:T(8,128)S(1)} collective-permute-done((f32[216,128]{1,0:T(8,128)S(1)}, f32[216,128]{1,0:T(8,128)S(1)}, u32[]{:S(2)}, u32[]{:S(2)}) %collective-permute-start.17) | collective-permute-done | bytes 110624 | tf_op jit(solution)/shard_map/ppermute | solution.py:402
  68.7 0.0 collective-permute-done.18.refs_3_
  68.7 0.0 collective-permute-done.19.refs_4_
  68.8 2.2 %shard_map.145 = f32[9,56,128]{2,1,0:T(8,128)} custom-call(f32[216,128]{1,0:T(8,128)S(1)} %collective-permute-done.15.refs_0_, f32[216,128]{1,0:T(8,128)S(1)} %collective-permute-done.16.refs_1_, f32[216,128]{1,0:T(8,128)S(1)} %collective-permute-done.17.refs_2_, f32[216,128]{1,0:T(8,128)S(1)} %collective-permute-done.18.refs_3_, ...), custom_call_target="tpu_custom_call" | custom-call | flops 10000000 | bytes 1048576 | tf_op jit(solution)/shard_map/pallas_call | solution.py:339
  (18 shorter events, 0.0 us)
Async XLA Ops:
  0.0 0.7 copy-start.12
  0.0 0.7 copy-start.11
  0.0 0.7 copy-start.15
  0.7 0.9 %copy-start = (f32[3,9,9,128]{3,0,2,1:T(4,128)S(1)}, f32[3,9,9,128]{3,0,2,1:T(4,128)}, u32[]{:S(2)}) copy-start(f32[3,9,9,128]{3,0,2,1:T(4,128)} %param.15) | copy-start | bytes 373252
  1.6 0.9 %copy-start.4 = (f32[56,9,128]{2,0,1:T(8,128)S(1)}, f32[56,9,128]{2,0,1:T(8,128)}, u32[]{:S(2)}) copy-start(f32[56,9,128]{2,0,1:T(8,128)} %param.14) | copy-start | bytes 774148
  2.6 0.9 %copy-start.7 = (f32[3,56,56]{2,1,0:T(8,128)S(1)}, f32[3,56,56]{2,1,0:T(8,128)}, u32[]{:S(2)}) copy-start(f32[3,56,56]{2,1,0:T(8,128)} %refs_2_.2) | copy-start | bytes 112900
  3.4 0.8 %copy-start.9 = (f32[4,21,56]{2,0,1:T(4,128)S(1)}, f32[4,21,56]{2,0,1:T(4,128)}, u32[]{:S(2)}) copy-start(f32[4,21,56]{2,0,1:T(4,128)} %param.18) | copy-start | bytes 56452
  4.2 14.8 %copy-start.6 = (f32[3,56,56]{2,1,0:T(8,128)S(1)}, f32[3,56,56]{2,1,0:T(8,128)}, u32[]{:S(2)}) copy-start(f32[3,56,56]{2,1,0:T(8,128)} %refs_0_.1) | copy-start | bytes 112900
  4.2 14.8 %copy-start.8 = (f32[4,56,21]{1,0,2:T(4,128)S(1)}, f32[4,56,21]{1,0,2:T(4,128)}, u32[]{:S(2)}) copy-start(f32[4,56,21]{1,0,2:T(4,128)} %param.19) | copy-start | bytes 56452
  4.2 14.8 %copy-start.13 = (s32[4,128]{1,0:T(4,128)S(1)}, s32[4,128]{1,0:T(4,128)}, u32[]{:S(2)}) copy-start(s32[4,128]{1,0:T(4,128)} %refs_3_.1) | copy-start | bytes 6148
  4.2 14.8 %copy-start.14 = (s32[4,128]{1,0:T(4,128)S(1)}, s32[4,128]{1,0:T(4,128)}, u32[]{:S(2)}) copy-start(s32[4,128]{1,0:T(4,128)} %refs_4_.1) | copy-start | bytes 6148
  4.2 16.8 %copy-start.3 = (f32[4,9,9,128]{3,0,2,1:T(4,128)S(1)}, f32[4,9,9,128]{3,0,2,1:T(4,128)}, u32[]{:S(2)}) copy-start(f32[4,9,9,128]{3,0,2,1:T(4,128)} %param.21) | copy-start | bytes 497668
  4.3 16.8 %copy-start.5 = (f32[56,9,128]{2,0,1:T(8,128)S(1)}, f32[56,9,128]{2,0,1:T(8,128)}, u32[]{:S(2)}) copy-start(f32[56,9,128]{2,0,1:T(8,128)} %param.14) | copy-start | bytes 774148
  10.3 10.8 %copy-start.1 = (f32[3,9,9,128]{3,0,2,1:T(4,128)S(1)}, f32[3,9,9,128]{3,0,2,1:T(4,128)}, u32[]{:S(2)}) copy-start(f32[3,9,9,128]{3,0,2,1:T(4,128)} %param.15) | copy-start | bytes 373252
  10.3 12.1 %collective-permute-start = (f32[216,128]{1,0:T(8,128)S(1)}, f32[216,128]{1,0:T(8,128)S(1)}, u32[]{:S(2)}, u32[]{:S(2)}) collective-permute-start(f32[216,128]{1,0:T(8,128)S(1)} %get-tuple-element.59), channel_id=1, source_target_pairs={{0,16},{16,0},{1,17},{17,1},{2,18},{18,2},{3,19},{19,3},{4,20},{20... | collective-permute-start | bytes 331784 | tf_op jit(solution)/shard_map/ppermute | solution.py:402
  13.3 9.0 %collective-permute-start.1 = (f32[216,128]{1,0:T(8,128)S(1)}, f32[216,128]{1,0:T(8,128)S(1)}, u32[]{:S(2)}, u32[]{:S(2)}) collective-permute-start(f32[216,128]{1,0:T(8,128)S(1)} %get-tuple-element.60), channel_id=1, source_target_pairs={{0,4},{4,0},{8,12},{12,8},{1,5},{5,1},{9,13},{13,9},{2,6},{6,2},{1... | collective-permute-start | bytes 331784 | tf_op jit(solution)/shard_map/ppermute | solution.py:402
  14.9 7.4 %collective-permute-start.2 = (f32[216,128]{1,0:T(8,128)S(1)}, f32[216,128]{1,0:T(8,128)S(1)}, u32[]{:S(2)}, u32[]{:S(2)}) collective-permute-start(f32[216,128]{1,0:T(8,128)S(1)} %get-tuple-element.61), channel_id=1, source_target_pairs={{4,8},{8,4},{12,0},{0,12},{5,9},{9,5},{13,1},{1,13},{6,10},{10,6},... | collective-permute-start | bytes 331784 | tf_op jit(solution)/shard_map/ppermute | solution.py:402
  17.4 5.0 %collective-permute-start.3 = (f32[216,128]{1,0:T(8,128)S(1)}, f32[216,128]{1,0:T(8,128)S(1)}, u32[]{:S(2)}, u32[]{:S(2)}) collective-permute-start(f32[216,128]{1,0:T(8,128)S(1)} %get-tuple-element.62), channel_id=1, source_target_pairs={{0,1},{1,0},{2,3},{3,2},{4,5},{5,4},{6,7},{7,6},{8,9},{9,8},{10,11... | collective-permute-start | bytes 331784 | tf_op jit(solution)/shard_map/ppermute | solution.py:402
  17.4 5.0 %collective-permute-start.4 = (f32[216,128]{1,0:T(8,128)S(1)}, f32[216,128]{1,0:T(8,128)S(1)}, u32[]{:S(2)}, u32[]{:S(2)}) collective-permute-start(f32[216,128]{1,0:T(8,128)S(1)} %get-tuple-element.63), channel_id=1, source_target_pairs={{1,2},{2,1},{3,0},{0,3},{5,6},{6,5},{7,4},{4,7},{9,10},{10,9},{11,... | collective-permute-start | bytes 331784 | tf_op jit(solution)/shard_map/ppermute | solution.py:402
  19.0 0.8 %copy-start.10 = (f32[3,21,21]{2,1,0:T(8,128)S(1)}, f32[3,21,21]{2,1,0:T(8,128)}, u32[]{:S(2)}) copy-start(f32[3,21,21]{2,1,0:T(8,128)} %refs_2_.3) | copy-start | bytes 15880
  21.0 1.3 %copy-start.2 = (f32[4,9,9,128]{3,0,2,1:T(4,128)S(1)}, f32[4,9,9,128]{3,0,2,1:T(4,128)}, u32[]{:S(2)}) copy-start(f32[4,9,9,128]{3,0,2,1:T(4,128)} %param.22) | copy-start | bytes 497668
  28.8 6.7 %collective-permute-start.5 = (f32[216,128]{1,0:T(8,128)S(1)}, f32[216,128]{1,0:T(8,128)S(1)}, u32[]{:S(2)}, u32[]{:S(2)}) collective-permute-start(f32[216,128]{1,0:T(8,128)S(1)} %get-tuple-element.78), channel_id=1, source_target_pairs={{0,16},{16,0},{1,17},{17,1},{2,18},{18,2},{3,19},{19,3},{4,20},{20... | collective-permute-start | bytes 331784 | tf_op jit(solution)/shard_map/ppermute | solution.py:402
  29.4 6.1 %collective-permute-start.6 = (f32[216,128]{1,0:T(8,128)S(1)}, f32[216,128]{1,0:T(8,128)S(1)}, u32[]{:S(2)}, u32[]{:S(2)}) collective-permute-start(f32[216,128]{1,0:T(8,128)S(1)} %get-tuple-element.79), channel_id=1, source_target_pairs={{0,4},{4,0},{8,12},{12,8},{1,5},{5,1},{9,13},{13,9},{2,6},{6,2},{1... | collective-permute-start | bytes 331784 | tf_op jit(solution)/shard_map/ppermute | solution.py:402
  30.1 7.6 %collective-permute-start.7 = (f32[216,128]{1,0:T(8,128)S(1)}, f32[216,128]{1,0:T(8,128)S(1)}, u32[]{:S(2)}, u32[]{:S(2)}) collective-permute-start(f32[216,128]{1,0:T(8,128)S(1)} %get-tuple-element.80), channel_id=1, source_target_pairs={{4,8},{8,4},{12,0},{0,12},{5,9},{9,5},{13,1},{1,13},{6,10},{10,6},... | collective-permute-start | bytes 331784 | tf_op jit(solution)/shard_map/ppermute | solution.py:402
  32.6 5.1 %collective-permute-start.8 = (f32[216,128]{1,0:T(8,128)S(1)}, f32[216,128]{1,0:T(8,128)S(1)}, u32[]{:S(2)}, u32[]{:S(2)}) collective-permute-start(f32[216,128]{1,0:T(8,128)S(1)} %get-tuple-element.81), channel_id=1, source_target_pairs={{0,1},{1,0},{2,3},{3,2},{4,5},{5,4},{6,7},{7,6},{8,9},{9,8},{10,11... | collective-permute-start | bytes 331784 | tf_op jit(solution)/shard_map/ppermute | solution.py:402
  32.6 5.1 %collective-permute-start.9 = (f32[216,128]{1,0:T(8,128)S(1)}, f32[216,128]{1,0:T(8,128)S(1)}, u32[]{:S(2)}, u32[]{:S(2)}) collective-permute-start(f32[216,128]{1,0:T(8,128)S(1)} %get-tuple-element.82), channel_id=1, source_target_pairs={{1,2},{2,1},{3,0},{0,3},{5,6},{6,5},{7,4},{4,7},{9,10},{10,9},{11,... | collective-permute-start | bytes 331784 | tf_op jit(solution)/shard_map/ppermute | solution.py:402
  44.3 6.9 %collective-permute-start.10 = (f32[216,128]{1,0:T(8,128)S(1)}, f32[216,128]{1,0:T(8,128)S(1)}, u32[]{:S(2)}, u32[]{:S(2)}) collective-permute-start(f32[216,128]{1,0:T(8,128)S(1)} %get-tuple-element.90), channel_id=1, source_target_pairs={{0,16},{16,0},{1,17},{17,1},{2,18},{18,2},{3,19},{19,3},{4,20},{20... | collective-permute-start | bytes 331784 | tf_op jit(solution)/shard_map/ppermute | solution.py:402
  45.9 5.4 %collective-permute-start.11 = (f32[216,128]{1,0:T(8,128)S(1)}, f32[216,128]{1,0:T(8,128)S(1)}, u32[]{:S(2)}, u32[]{:S(2)}) collective-permute-start(f32[216,128]{1,0:T(8,128)S(1)} %get-tuple-element.91), channel_id=1, source_target_pairs={{0,4},{4,0},{8,12},{12,8},{1,5},{5,1},{9,13},{13,9},{2,6},{6,2},{1... | collective-permute-start | bytes 331784 | tf_op jit(solution)/shard_map/ppermute | solution.py:402
  46.6 6.8 %collective-permute-start.12 = (f32[216,128]{1,0:T(8,128)S(1)}, f32[216,128]{1,0:T(8,128)S(1)}, u32[]{:S(2)}, u32[]{:S(2)}) collective-permute-start(f32[216,128]{1,0:T(8,128)S(1)} %get-tuple-element.92), channel_id=1, source_target_pairs={{4,8},{8,4},{12,0},{0,12},{5,9},{9,5},{13,1},{1,13},{6,10},{10,6},... | collective-permute-start | bytes 331784 | tf_op jit(solution)/shard_map/ppermute | solution.py:402
  48.2 5.2 %collective-permute-start.13 = (f32[216,128]{1,0:T(8,128)S(1)}, f32[216,128]{1,0:T(8,128)S(1)}, u32[]{:S(2)}, u32[]{:S(2)}) collective-permute-start(f32[216,128]{1,0:T(8,128)S(1)} %get-tuple-element.93), channel_id=1, source_target_pairs={{0,1},{1,0},{2,3},{3,2},{4,5},{5,4},{6,7},{7,6},{8,9},{9,8},{10,11... | collective-permute-start | bytes 331784 | tf_op jit(solution)/shard_map/ppermute | solution.py:402
  48.2 5.2 %collective-permute-start.14 = (f32[216,128]{1,0:T(8,128)S(1)}, f32[216,128]{1,0:T(8,128)S(1)}, u32[]{:S(2)}, u32[]{:S(2)}) collective-permute-start(f32[216,128]{1,0:T(8,128)S(1)} %get-tuple-element.94), channel_id=1, source_target_pairs={{1,2},{2,1},{3,0},{0,3},{5,6},{6,5},{7,4},{4,7},{9,10},{10,9},{11,... | collective-permute-start | bytes 331784 | tf_op jit(solution)/shard_map/ppermute | solution.py:402
  60.2 6.2 %collective-permute-start.15 = (f32[216,128]{1,0:T(8,128)S(1)}, f32[216,128]{1,0:T(8,128)S(1)}, u32[]{:S(2)}, u32[]{:S(2)}) collective-permute-start(f32[216,128]{1,0:T(8,128)S(1)} %get-tuple-element.102), channel_id=1, source_target_pairs={{0,16},{16,0},{1,17},{17,1},{2,18},{18,2},{3,19},{19,3},{4,20},{20... | collective-permute-start | bytes 331784 | tf_op jit(solution)/shard_map/ppermute | solution.py:402
  60.7 5.7 %collective-permute-start.16 = (f32[216,128]{1,0:T(8,128)S(1)}, f32[216,128]{1,0:T(8,128)S(1)}, u32[]{:S(2)}, u32[]{:S(2)}) collective-permute-start(f32[216,128]{1,0:T(8,128)S(1)} %get-tuple-element.103), channel_id=1, source_target_pairs={{0,4},{4,0},{8,12},{12,8},{1,5},{5,1},{9,13},{13,9},{2,6},{6,2},{1... | collective-permute-start | bytes 331784 | tf_op jit(solution)/shard_map/ppermute | solution.py:402
  62.1 6.7 %collective-permute-start.17 = (f32[216,128]{1,0:T(8,128)S(1)}, f32[216,128]{1,0:T(8,128)S(1)}, u32[]{:S(2)}, u32[]{:S(2)}) collective-permute-start(f32[216,128]{1,0:T(8,128)S(1)} %get-tuple-element.104), channel_id=1, source_target_pairs={{4,8},{8,4},{12,0},{0,12},{5,9},{9,5},{13,1},{1,13},{6,10},{10,6},... | collective-permute-start | bytes 331784 | tf_op jit(solution)/shard_map/ppermute | solution.py:402
  63.6 5.2 %collective-permute-start.18 = (f32[216,128]{1,0:T(8,128)S(1)}, f32[216,128]{1,0:T(8,128)S(1)}, u32[]{:S(2)}, u32[]{:S(2)}) collective-permute-start(f32[216,128]{1,0:T(8,128)S(1)} %get-tuple-element.105), channel_id=1, source_target_pairs={{0,1},{1,0},{2,3},{3,2},{4,5},{5,4},{6,7},{7,6},{8,9},{9,8},{10,11... | collective-permute-start | bytes 331784 | tf_op jit(solution)/shard_map/ppermute | solution.py:402
  63.6 5.2 %collective-permute-start.19 = (f32[216,128]{1,0:T(8,128)S(1)}, f32[216,128]{1,0:T(8,128)S(1)}, u32[]{:S(2)}, u32[]{:S(2)}) collective-permute-start(f32[216,128]{1,0:T(8,128)S(1)} %get-tuple-element.106), channel_id=1, source_target_pairs={{1,2},{2,1},{3,0},{0,3},{5,6},{6,5},{7,4},{4,7},{9,10},{10,9},{11,... | collective-permute-start | bytes 331784 | tf_op jit(solution)/shard_map/ppermute | solution.py:402
where the time goes:
time: 71.3 us; the launch traced here: 71 us
  Pallas kernels  34.3 us (48%)
  starting transfers between devices  24.6 us (35%)
  waiting for transfers between devices  6.76 us (9%)
  local copies, waits for them, and re-layouts  5.02 us (7%)
    pallas_call x10, Pallas kernels, call(): pl.pallas_call(body, out_shape=[jax.ShapeDtypeStruct(shape, kind) for sha...  34.3 us
    ppermute x20, starting transfers between devices, trade(): lax.ppermute(value, AXES[number], partners(size, kind))  24.6 us
    ppermute x20, waiting for transfers between devices, trade(): lax.ppermute(value, AXES[number], partners(size, kind))  6.76 us
    unnamed x32, local copies, waits for them, and re-layouts  5.02 us
  transfers between devices with their start and end apart: 20, of which 4 were waited for; matrix products, arithmetic and copies ran while one was open for 0% of the time, Pallas kernels for 9%

commit v1 on v0

--- a/solution.py
+++ b/solution.py
@@ -46,16 +46,25 @@
     return tuple(plan)
 
 
-def partners(size, kind):
-    if kind == "up":
-        return [(i, (i + 1) % size) for i in range(size)]
-    if kind == "down":
-        return [(i, (i - 1) % size) for i in range(size)]
-    first = 0 if kind == "pair0" else 1
+def partners(sizes, entry):
+    number, size, kind = entry
+    spare = [other for other in (2, 0, 1) if other != number and sizes[other] % 2 == 0]
     pairs = []
-    for i in range(first, size + first, 2):
-        low, high = i % size, (i + 1) % size
-        pairs += [(low, high), (high, low)]
+    for flat in range(math.prod(sizes)):
+        place = [flat // (sizes[1] * sizes[2]), flat // sizes[2] % sizes[1], flat % sizes[2]]
+        source = flat
+        here = place[number]
+        if kind in ("up", "down"):
+            place[number] = (here + (1 if kind == "up" else -1)) % size
+        elif kind == "pair0":
+            place[number] = here ^ 1
+        elif 0 < here < size - 1:
+            place[number] = ((here + 1) ^ 1) - 1
+        elif spare:
+            place[spare[0]] ^= 1
+        else:
+            place[number] = size - 1 - here
+        pairs.append((source, (place[0] * sizes[1] + place[1]) * sizes[2] + place[2]))
     return pairs
 
 
@@ -132,8 +141,8 @@
 
 def contract(z, mixed, jacobians, first, rows):
     totals = [None] * z.quantities
-    for d in range(3):
-        for q in range(z.quantities):
+    for q in range(z.quantities):
+        for d in range(3):
             start = d * z.basis + first
             value = mixed[start : start + rows, q * z.elements : (q + 1) * z.elements]
             for p in range(z.quantities):
@@ -189,20 +198,30 @@
 
 def first_kernel(z, *refs):
     count = len(z.plan)
-    solution, jacobians, stiffness, projection, cluster, send_faces, counts = refs[:7]
     outgoing = refs[7 : 7 + count]
     table, faces, moments, stiff, project, send_hot = refs[7 + count : 13 + count]
-    rhs, mixed, total, weights, wide_stiff, wide_project = refs[13 + count :]
+    rhs, mixed, total, weights, wide_stiff, wide_project = refs[13 + count : 19 + count]
+    held, arrived = refs[19 + count : 26 + count], refs[26 + count]
+    copies = [pltpu.make_async_copy(refs[n], held[n], arrived.at[n]) for n in range(7)]
+    for n in (5, 6, 2, 3, 4, 0, 1):
+        copies[n].start()
+    solution, jacobians, stiffness, projection, cluster, send_faces, counts = held
     b = z.basis
-    stiff[...] = left_parts(wide_stiff, [(d * b, 0, -stiffness[d]) for d in range(3)], z.padded)
-    project[...] = left_parts(
-        wide_project, [(j * z.face_rows, 0, projection[:, j, :]) for j in range(z.faces)], z.padded
-    )
+    for n in (5, 6):
+        copies[n].wait()
     slot = lax.broadcasted_iota(jnp.int32, (1, z.slots), 1)
     for t, entry in enumerate(z.plan):
         chosen = lists_of(entry)[0]
         wanted = jnp.where(slot < counts[0, chosen], send_faces[pl.ds(chosen, 1), :], -1)
         send_hot[:, t * z.slots : (t + 1) * z.slots] = one_hot((z.face_total, z.slots), wanted, 0)
+    for n in (2, 3, 4):
+        copies[n].wait()
+    stiff[...] = left_parts(wide_stiff, [(d * b, 0, -stiffness[d]) for d in range(3)], z.padded)
+    project[...] = left_parts(
+        wide_project, [(j * z.face_rows, 0, projection[:, j, :]) for j in range(z.faces)], z.padded
+    )
+    for n in (0, 1):
+        copies[n].wait()
     predict(
         z, 0, cluster, lambda q, k, n: solution[q, k : k + n, :], jacobians, stiff, project, send_hot,
         outgoing, table, faces, moments, rhs, mixed, total, weights,
@@ -332,16 +351,14 @@
         advanced[q] = partial[q] - flux[:, q * e : (q + 1) * e]
 
 
-def call(body, outs, scratch, cost, arguments, scalars=()):
-    in_specs = [
-        pl.BlockSpec(memory_space=pltpu.SMEM if n in scalars else pltpu.VMEM) for n in range(len(arguments))
-    ]
+def call(body, outs, scratch, cost, arguments, space=pltpu.VMEM, more=()):
+    in_specs = [pl.BlockSpec(memory_space=space)] * len(arguments)
     return pl.pallas_call(
         body,
         out_shape=[jax.ShapeDtypeStruct(shape, kind) for shape, kind in outs],
         in_specs=in_specs,
         out_specs=[pl.BlockSpec(memory_space=pltpu.VMEM)] * len(outs),
-        scratch_shapes=[pltpu.VMEM(shape, kind) for shape, kind in scratch],
+        scratch_shapes=[*(pltpu.VMEM(shape, kind) for shape, kind in scratch), *more],
         cost_estimate=pl.CostEstimate(flops=cost, bytes_accessed=1 << 20, transcendentals=0),
         compiler_params=pltpu.CompilerParams(vmem_limit_bytes=24 << 20),
     )(*arguments)
@@ -366,6 +383,7 @@
 ):
     z = Sizes(solution, face_project, send_faces, plan)
     count = len(plan)
+    sizes = [lax.axis_size(axis) for axis in AXES]
     state = solution.transpose(1, 0, 2)
     jacobians = jacobians.transpose(1, 2, 0, 3)
     local_solver = local_solver.transpose(1, 2, 0, 3)
@@ -399,17 +417,22 @@
 
     def trade(outgoing):
         return [
-            lax.ppermute(value, AXES[number], partners(size, kind))
-            for value, (number, size, kind) in zip(outgoing, plan)
+            lax.ppermute(value, AXES, partners(sizes, entry)) for value, entry in zip(outgoing, plan)
         ]
 
+    first_arguments = (state, jacobians, derivative_stiffness, projection, cluster, send_faces, counts)
     results = call(
         functools.partial(first_kernel, z),
         [block] * count + [table, faces, moments, stiff, project, send_hot],
         [moments, mixed, field, weights, wide(stiff), wide(project)],
         10_000_000,
-        (state, jacobians, derivative_stiffness, projection, cluster, send_faces, counts),
-        scalars=(6,),
+        first_arguments,
+        space=pltpu.HBM,
+        more=[
+            *(pltpu.VMEM(value.shape, value.dtype) for value in first_arguments[:-1]),
+            pltpu.SMEM(counts.shape, counts.dtype),
+            pltpu.SemaphoreType.DMA((len(first_arguments),)),
+        ],
     )
     outgoing = results[:count]
     table_now, faces_now, moments_now, stiff_left, project_left, send_matrix = results[count:]

time: 71.3 us -> 65.9 us (0.924)
  starting transfers between devices: 24.6 us -> 17.5 us
  waiting for transfers between devices: 6.76 us -> 7.81 us
    ppermute x20, starting transfers between devices: 24.6 us -> 17.5 us  [trade(): lax.ppermute(value, AXES, partners(sizes, entry))]
    ppermute x20, waiting for transfers between devices: 6.76 us -> 7.81 us  [trade(): lax.ppermute(value, AXES, partners(sizes, entry))]
  transfers between devices with their start and end apart: 20 -> 20, of which waited for: 4 -> 7; matrix products, arithmetic and copies ran while one was open for 0% -> 0% of each run, Pallas kernels for 9% -> 10%
where the time goes in v1:
time: 65.9 us; the launch traced here: 65.6 us
  Pallas kernels  35 us (53%)
  starting transfers between devices  17.5 us (27%)
  waiting for transfers between devices  7.81 us (12%)
  local copies, waits for them, and re-layouts  5.02 us (8%)
    pallas_call x10, Pallas kernels, call(): pl.pallas_call(body, out_shape=[jax.ShapeDtypeStruct(shape, kind) for sha...  35 us
    ppermute x20, starting transfers between devices, trade(): lax.ppermute(value, AXES, partners(sizes, entry))  17.5 us
    ppermute x20, waiting for transfers between devices, trade(): lax.ppermute(value, AXES, partners(sizes, entry))  7.81 us
    unnamed x32, local copies, waits for them, and re-layouts  5.02 us
  transfers between devices with their start and end apart: 20, of which 7 were waited for; matrix products, arithmetic and copies ran while one was open for 0% of the time, Pallas kernels for 10%

profile of v1, /device:TPU:0, one launch (start us, length us, event | category | flops | bytes accessed | tf_op | source)
XLA Modules:
  0.0 65.6 jit_solution(15925104462238454879)
XLA Ops:
  0.0 0.7 %copy-done.12 = s32[6,128]{1,0:T(8,128)S(1)} copy-done((s32[6,128]{1,0:T(8,128)S(1)}, s32[6,128]{1,0:T(8,128)}, u32[]{:S(2)}) %copy-start.12) | copy-done | bytes 3096
  0.7 0.0 copy-done.11
  0.7 0.0 copy-done.15
  0.7 0.9 %copy-done = f32[3,9,9,128]{3,0,2,1:T(4,128)S(1)} copy-done((f32[3,9,9,128]{3,0,2,1:T(4,128)S(1)}, f32[3,9,9,128]{3,0,2,1:T(4,128)}, u32[]{:S(2)}) %copy-start) | copy-done | bytes 124440
  1.6 0.9 %copy-done.4 = f32[56,9,128]{2,0,1:T(8,128)S(1)} copy-done((f32[56,9,128]{2,0,1:T(8,128)S(1)}, f32[56,9,128]{2,0,1:T(8,128)}, u32[]{:S(2)}) %copy-start.4) | copy-done | bytes 258072
  2.6 0.9 %copy-done.7 = f32[3,56,56]{2,1,0:T(8,128)S(1)} copy-done((f32[3,56,56]{2,1,0:T(8,128)S(1)}, f32[3,56,56]{2,1,0:T(8,128)}, u32[]{:S(2)}) %copy-start.7) | copy-done | bytes 37656
  3.5 0.8 %copy-done.9 = f32[4,21,56]{2,0,1:T(4,128)S(1)} copy-done((f32[4,21,56]{2,0,1:T(4,128)S(1)}, f32[4,21,56]{2,0,1:T(4,128)}, u32[]{:S(2)}) %copy-start.9) | copy-done | bytes 18840
  4.2 0.0 copy-start.3
  4.3 6.0 %shard_map.136 = (f32[216,128]{1,0:T(8,128)S(1)}, f32[216,128]{1,0:T(8,128)S(1)}, f32[216,128]{1,0:T(8,128)S(1)}, f32[216,128]{1,0:T(8,128)S(1)}, f32[216,128]{1...) custom-call(f32[9,56,128]{2,1,0:T(8,128)S(1)} %bitcast.25, ...), custom_call_target="tpu_custom_call" | custom-call | flops 10000000 | bytes 1048576 | tf_op jit(solution)/shard_map/pallas_call | solution.py:356
  10.3 0.0 copy-start.1
  10.3 3.1 %collective-permute-start = (f32[216,128]{1,0:T(8,128)S(1)}, f32[216,128]{1,0:T(8,128)S(1)}, u32[]{:S(2)}, u32[]{:S(2)}) collective-permute-start(f32[216,128]{1,0:T(8,128)S(1)} %get-tuple-element.59), channel_id=1, source_target_pairs={{0,16},{1,17},{2,18},{3,19},{4,20},{5,21},{6,22},{7,23},{8,24},{9,... | collective-permute-start | bytes 331784 | tf_op jit(solution)/shard_map/ppermute | solution.py:420
  13.4 1.6 %collective-permute-start.1 = (f32[216,128]{1,0:T(8,128)S(1)}, f32[216,128]{1,0:T(8,128)S(1)}, u32[]{:S(2)}, u32[]{:S(2)}) collective-permute-start(f32[216,128]{1,0:T(8,128)S(1)} %get-tuple-element.60), channel_id=1, source_target_pairs={{0,4},{1,5},{2,6},{3,7},{4,0},{5,1},{6,2},{7,3},{8,12},{9,13},{10,... | collective-permute-start | bytes 331784 | tf_op jit(solution)/shard_map/ppermute | solution.py:420
  15.0 0.0 collective-permute-start.2
  15.0 0.5 collective-permute-start.3
  15.5 0.5 collective-permute-start.4
  16.0 0.0 copy-done.6
  16.0 0.0 copy-done.13
  16.0 0.0 copy-start.10
  16.0 0.8 %copy-done.10 = f32[3,21,21]{2,1,0:T(8,128)S(1)} copy-done((f32[3,21,21]{2,1,0:T(8,128)S(1)}, f32[3,21,21]{2,1,0:T(8,128)}, u32[]{:S(2)}) %copy-start.10) | copy-done | bytes 5316
  16.7 1.2 %shard_map.137 = (bf16[168,192]{1,0:T(8,128)(2,1)S(1)}, bf16[56,288]{1,0:T(8,128)(2,1)S(1)}, bf16[56,864]{1,0:T(8,128)(2,1)S(1)}, bf16[3,96,128]{2,1,0:T(8,128)(...) custom-call(f32[3,56,56]{2,1,0:T(8,128)S(1)} %copy-done.6, f32[21,4,56]{2,1,0:T(4,128)S(1)} %bitcast.28, ...), custom_call_target="tpu_custom_call" | custom-call | flops 1000000 | bytes 1048576 | tf_op jit(solution)/shard_map/pallas_call | solution.py:356
  18.0 0.0 copy-start.2
  18.0 1.3 %shard_map.138 = (f32[216,512]{1,0:T(8,128)S(1)}, f32[9,56,128]{2,1,0:T(8,128)S(1)}) custom-call(f32[9,56,128]{2,1,0:T(8,128)S(1)} %bitcast.26, bf16[448,512]{1,0:T(8,128)(2,1)S(1)} %get-tuple-element.64.table, f32[96,1152]{1,0:T(8,128)S(1)} %get-tuple-element.65.faces, bf16[192,1152]{1,0:T(8,128)(2,1)S(1)} %get-tuple-element.66.moments, ...), custom_call_target="tpu_custom_call" | custom-call | flops 10000000 | bytes 1048576 | tf_op jit(solution)/shard_map/pallas_call | solution.py:356
  19.3 0.0 collective-permute-done.refs_0_
  19.3 0.0 collective-permute-done.1.refs_1_
  19.3 0.0 collective-permute-done.2.refs_2_
  19.4 0.0 collective-permute-done.3.refs_3_
  19.4 0.8 %collective-permute-done.4.refs_4_ = f32[216,128]{1,0:T(8,128)S(1)} collective-permute-done((f32[216,128]{1,0:T(8,128)S(1)}, f32[216,128]{1,0:T(8,128)S(1)}, u32[]{:S(2)}, u32[]{:S(2)}) %collective-permute-start.4) | collective-permute-done | bytes 110624 | tf_op jit(solution)/shard_map/ppermute | solution.py:420
  20.2 6.6 %shard_map.139 = (f32[216,128]{1,0:T(8,128)S(1)}, f32[216,128]{1,0:T(8,128)S(1)}, f32[216,128]{1,0:T(8,128)S(1)}, f32[216,128]{1,0:T(8,128)S(1)}, f32[216,128]{1...) custom-call(f32[216,128]{1,0:T(8,128)S(1)} %collective-permute-done., ...), custom_call_target="tpu_custom_call" | custom-call | flops 10000000 | bytes 1048576 | tf_op jit(solution)/shard_map/pallas_call | solution.py:356
  26.8 0.8 %collective-permute-start.5 = (f32[216,128]{1,0:T(8,128)S(1)}, f32[216,128]{1,0:T(8,128)S(1)}, u32[]{:S(2)}, u32[]{:S(2)}) collective-permute-start(f32[216,128]{1,0:T(8,128)S(1)} %get-tuple-element.78), channel_id=1, source_target_pairs={{0,16},{1,17},{2,18},{3,19},{4,20},{5,21},{6,22},{7,23},{8,24},{9,... | collective-permute-start | bytes 331784 | tf_op jit(solution)/shard_map/ppermute | solution.py:420
  27.6 2.6 %collective-permute-start.6 = (f32[216,128]{1,0:T(8,128)S(1)}, f32[216,128]{1,0:T(8,128)S(1)}, u32[]{:S(2)}, u32[]{:S(2)}) collective-permute-start(f32[216,128]{1,0:T(8,128)S(1)} %get-tuple-element.79), channel_id=1, source_target_pairs={{0,4},{1,5},{2,6},{3,7},{4,0},{5,1},{6,2},{7,3},{8,12},{9,13},{10,... | collective-permute-start | bytes 331784 | tf_op jit(solution)/shard_map/ppermute | solution.py:420
  30.2 0.0 collective-permute-start.7
  30.2 0.5 collective-permute-start.8
  30.7 1.3 %collective-permute-start.9 = (f32[216,128]{1,0:T(8,128)S(1)}, f32[216,128]{1,0:T(8,128)S(1)}, u32[]{:S(2)}, u32[]{:S(2)}) collective-permute-start(f32[216,128]{1,0:T(8,128)S(1)} %get-tuple-element.82), channel_id=1, source_target_pairs={{0,16},{1,2},{2,1},{3,19},{4,20},{5,6},{6,5},{7,23},{8,24},{9,10},... | collective-permute-start | bytes 331784 | tf_op jit(solution)/shard_map/ppermute | solution.py:420
  32.0 1.3 %shard_map.140 = (f32[216,512]{1,0:T(8,128)S(1)}, f32[9,56,128]{2,1,0:T(8,128)S(1)}) custom-call(f32[9,56,128]{2,1,0:T(8,128)S(1)} %get-tuple-element.83.running, bf16[448,512]{1,0:T(8,128)(2,1)S(1)} %get-tuple-element.84.table, f32[96,1152]{1,0:T(8,128)S(1)} %get-tuple-element.85.faces, bf16[192,1152]{1,0:T(8,128)(2,1)S(1)} %get-tuple-element.86.moments, ...), custom_call_target="tpu_custom_call" | custom-call | flops 10000000 | bytes 1048576 | tf_op jit(solution)/shard_map/pallas_call | solution.py:356
  33.3 0.0 collective-permute-done.5.refs_0_
  33.4 0.0 collective-permute-done.6.refs_1_
  33.4 0.0 collective-permute-done.7.refs_2_
  33.4 0.0 collective-permute-done.8.refs_3_
  33.4 2.1 %collective-permute-done.9.refs_4_ = f32[216,128]{1,0:T(8,128)S(1)} collective-permute-done((f32[216,128]{1,0:T(8,128)S(1)}, f32[216,128]{1,0:T(8,128)S(1)}, u32[]{:S(2)}, u32[]{:S(2)}) %collective-permute-start.9) | collective-permute-done | bytes 110624 | tf_op jit(solution)/shard_map/ppermute | solution.py:420
  35.5 6.8 %shard_map.141 = (f32[216,128]{1,0:T(8,128)S(1)}, f32[216,128]{1,0:T(8,128)S(1)}, f32[216,128]{1,0:T(8,128)S(1)}, f32[216,128]{1,0:T(8,128)S(1)}, f32[216,128]{1...) custom-call(f32[216,128]{1,0:T(8,128)S(1)} %collective-permute-done., ...), custom_call_target="tpu_custom_call" | custom-call | flops 10000000 | bytes 1048576 | tf_op jit(solution)/shard_map/pallas_call | solution.py:356
  42.2 1.4 %collective-permute-start.10 = (f32[216,128]{1,0:T(8,128)S(1)}, f32[216,128]{1,0:T(8,128)S(1)}, u32[]{:S(2)}, u32[]{:S(2)}) collective-permute-start(f32[216,128]{1,0:T(8,128)S(1)} %get-tuple-element.90), channel_id=1, source_target_pairs={{0,16},{1,17},{2,18},{3,19},{4,20},{5,21},{6,22},{7,23},{8,24},{9,... | collective-permute-start | bytes 331784 | tf_op jit(solution)/shard_map/ppermute | solution.py:420
  43.6 0.5 collective-permute-start.11
  44.1 0.0 collective-permute-start.12
  44.1 0.5 collective-permute-start.13
  44.6 0.7 %collective-permute-start.14 = (f32[216,128]{1,0:T(8,128)S(1)}, f32[216,128]{1,0:T(8,128)S(1)}, u32[]{:S(2)}, u32[]{:S(2)}) collective-permute-start(f32[216,128]{1,0:T(8,128)S(1)} %get-tuple-element.94), channel_id=1, source_target_pairs={{0,16},{1,2},{2,1},{3,19},{4,20},{5,6},{6,5},{7,23},{8,24},{9,10},... | collective-permute-start | bytes 331784 | tf_op jit(solution)/shard_map/ppermute | solution.py:420
  45.3 1.3 %shard_map.142 = (f32[216,512]{1,0:T(8,128)S(1)}, f32[9,56,128]{2,1,0:T(8,128)S(1)}) custom-call(f32[9,56,128]{2,1,0:T(8,128)S(1)} %get-tuple-element.95.running, bf16[448,512]{1,0:T(8,128)(2,1)S(1)} %get-tuple-element.96.table, f32[96,1152]{1,0:T(8,128)S(1)} %get-tuple-element.97.faces, bf16[192,1152]{1,0:T(8,128)(2,1)S(1)} %get-tuple-element.98.moments, ...), custom_call_target="tpu_custom_call" | custom-call | flops 10000000 | bytes 1048576 | tf_op jit(solution)/shard_map/pallas_call | solution.py:356
  46.6 0.5 collective-permute-done.10.refs_0_
  47.1 1.3 %collective-permute-done.11.refs_1_ = f32[216,128]{1,0:T(8,128)S(1)} collective-permute-done((f32[216,128]{1,0:T(8,128)S(1)}, f32[216,128]{1,0:T(8,128)S(1)}, u32[]{:S(2)}, u32[]{:S(2)}) %collective-permute-start.11) | collective-permute-done | bytes 110624 | tf_op jit(solution)/shard_map/ppermute | solution.py:420
  48.4 0.0 collective-permute-done.12.refs_2_
  48.4 0.0 collective-permute-done.13.refs_3_
  48.4 1.0 %collective-permute-done.14.refs_4_ = f32[216,128]{1,0:T(8,128)S(1)} collective-permute-done((f32[216,128]{1,0:T(8,128)S(1)}, f32[216,128]{1,0:T(8,128)S(1)}, u32[]{:S(2)}, u32[]{:S(2)}) %collective-permute-start.14) | collective-permute-done | bytes 110624 | tf_op jit(solution)/shard_map/ppermute | solution.py:420
  49.4 7.0 %shard_map.143 = (f32[216,128]{1,0:T(8,128)S(1)}, f32[216,128]{1,0:T(8,128)S(1)}, f32[216,128]{1,0:T(8,128)S(1)}, f32[216,128]{1,0:T(8,128)S(1)}, f32[216,128]{1...) custom-call(f32[216,128]{1,0:T(8,128)S(1)} %collective-permute-done., ...), custom_call_target="tpu_custom_call" | custom-call | flops 10000000 | bytes 1048576 | tf_op jit(solution)/shard_map/pallas_call | solution.py:356
  56.3 0.7 %collective-permute-start.15 = (f32[216,128]{1,0:T(8,128)S(1)}, f32[216,128]{1,0:T(8,128)S(1)}, u32[]{:S(2)}, u32[]{:S(2)}) collective-permute-start(f32[216,128]{1,0:T(8,128)S(1)} %get-tuple-element.102), channel_id=1, source_target_pairs={{0,16},{1,17},{2,18},{3,19},{4,20},{5,21},{6,22},{7,23},{8,24},{9,... | collective-permute-start | bytes 331784 | tf_op jit(solution)/shard_map/ppermute | solution.py:420
  57.0 1.1 %collective-permute-start.16 = (f32[216,128]{1,0:T(8,128)S(1)}, f32[216,128]{1,0:T(8,128)S(1)}, u32[]{:S(2)}, u32[]{:S(2)}) collective-permute-start(f32[216,128]{1,0:T(8,128)S(1)} %get-tuple-element.103), channel_id=1, source_target_pairs={{0,4},{1,5},{2,6},{3,7},{4,0},{5,1},{6,2},{7,3},{8,12},{9,13},{10,... | collective-permute-start | bytes 331784 | tf_op jit(solution)/shard_map/ppermute | solution.py:420
  58.1 0.0 collective-permute-start.17
  58.1 0.5 collective-permute-start.18
  58.6 1.3 %collective-permute-start.19 = (f32[216,128]{1,0:T(8,128)S(1)}, f32[216,128]{1,0:T(8,128)S(1)}, u32[]{:S(2)}, u32[]{:S(2)}) collective-permute-start(f32[216,128]{1,0:T(8,128)S(1)} %get-tuple-element.106), channel_id=1, source_target_pairs={{0,16},{1,2},{2,1},{3,19},{4,20},{5,6},{6,5},{7,23},{8,24},{9,10},... | collective-permute-start | bytes 331784 | tf_op jit(solution)/shard_map/ppermute | solution.py:420
  59.9 1.3 %shard_map.144 = (f32[216,512]{1,0:T(8,128)S(1)}, f32[9,56,128]{2,1,0:T(8,128)S(1)}) custom-call(f32[9,56,128]{2,1,0:T(8,128)S(1)} %get-tuple-element.107.running, bf16[448,512]{1,0:T(8,128)(2,1)S(1)} %get-tuple-element.108.table, f32[96,1152]{1,0:T(8,128)S(1)} %get-tuple-element.109.faces, bf16[192,1152]{1,0:T(8,128)(2,1)S(1)} %get-tuple-element.110.moments, ...), custom_call_target="tpu_custom_call" | custom-call | flops 10000000 | bytes 1048576 | tf_op jit(solution)/shard_map/pallas_call | solution.py:356
  61.2 0.0 collective-permute-done.15.refs_0_
  61.2 0.5 collective-permute-done.16.refs_1_
  61.8 0.0 collective-permute-done.17.refs_2_
  61.8 0.0 collective-permute-done.18.refs_3_
  61.8 1.6 %collective-permute-done.19.refs_4_ = f32[216,128]{1,0:T(8,128)S(1)} collective-permute-done((f32[216,128]{1,0:T(8,128)S(1)}, f32[216,128]{1,0:T(8,128)S(1)}, u32[]{:S(2)}, u32[]{:S(2)}) %collective-permute-start.19) | collective-permute-done | bytes 110624 | tf_op jit(solution)/shard_map/ppermute | solution.py:420
  63.3 2.2 %shard_map.145 = f32[9,56,128]{2,1,0:T(8,128)} custom-call(f32[216,128]{1,0:T(8,128)S(1)} %collective-permute-done.15.refs_0_, f32[216,128]{1,0:T(8,128)S(1)} %collective-permute-done.16.refs_1_, f32[216,128]{1,0:T(8,128)S(1)} %collective-permute-done.17.refs_2_, f32[216,128]{1,0:T(8,128)S(1)} %collective-permute-done.18.refs_3_, ...), custom_call_target="tpu_custom_call" | custom-call | flops 10000000 | bytes 1048576 | tf_op jit(solution)/shard_map/pallas_call | solution.py:356
  (18 shorter events, 0.0 us)
Async XLA Ops:
  0.0 0.7 %copy-start.12 = (s32[6,128]{1,0:T(8,128)S(1)}, s32[6,128]{1,0:T(8,128)}, u32[]{:S(2)}) copy-start(s32[6,128]{1,0:T(8,128)} %refs_5_.1) | copy-start | bytes 9220
  0.0 0.7 %copy-start.11 = (s32[128]{0:T(128)S(1)}, s32[128]{0:T(128)}, u32[]{:S(2)}) copy-start(s32[128]{0:T(128)} %param.23) | copy-start | bytes 1540
  0.0 0.7 %copy-start.15 = (s32[6,1]{0,1:T(1,128)S(1)}, s32[6,1]{0,1:T(1,128)}, u32[]{:S(2)}) copy-start(s32[6,1]{0,1:T(1,128)} %param.27) | copy-start | bytes 76
  0.7 0.9 %copy-start = (f32[3,9,9,128]{3,0,2,1:T(4,128)S(1)}, f32[3,9,9,128]{3,0,2,1:T(4,128)}, u32[]{:S(2)}) copy-start(f32[3,9,9,128]{3,0,2,1:T(4,128)} %param.15) | copy-start | bytes 373252
  1.6 0.9 %copy-start.4 = (f32[56,9,128]{2,0,1:T(8,128)S(1)}, f32[56,9,128]{2,0,1:T(8,128)}, u32[]{:S(2)}) copy-start(f32[56,9,128]{2,0,1:T(8,128)} %param.14) | copy-start | bytes 774148
  2.6 0.9 %copy-start.7 = (f32[3,56,56]{2,1,0:T(8,128)S(1)}, f32[3,56,56]{2,1,0:T(8,128)}, u32[]{:S(2)}) copy-start(f32[3,56,56]{2,1,0:T(8,128)} %refs_2_.2) | copy-start | bytes 112900
  3.4 0.8 %copy-start.9 = (f32[4,21,56]{2,0,1:T(4,128)S(1)}, f32[4,21,56]{2,0,1:T(4,128)}, u32[]{:S(2)}) copy-start(f32[4,21,56]{2,0,1:T(4,128)} %param.18) | copy-start | bytes 56452
  4.2 11.7 %copy-start.6 = (f32[3,56,56]{2,1,0:T(8,128)S(1)}, f32[3,56,56]{2,1,0:T(8,128)}, u32[]{:S(2)}) copy-start(f32[3,56,56]{2,1,0:T(8,128)} %refs_0_.1) | copy-start | bytes 112900
  4.2 11.7 %copy-start.8 = (f32[4,56,21]{1,0,2:T(4,128)S(1)}, f32[4,56,21]{1,0,2:T(4,128)}, u32[]{:S(2)}) copy-start(f32[4,56,21]{1,0,2:T(4,128)} %param.19) | copy-start | bytes 56452
  4.2 11.7 %copy-start.13 = (s32[4,128]{1,0:T(4,128)S(1)}, s32[4,128]{1,0:T(4,128)}, u32[]{:S(2)}) copy-start(s32[4,128]{1,0:T(4,128)} %refs_3_.1) | copy-start | bytes 6148
  4.2 11.7 %copy-start.14 = (s32[4,128]{1,0:T(4,128)S(1)}, s32[4,128]{1,0:T(4,128)}, u32[]{:S(2)}) copy-start(s32[4,128]{1,0:T(4,128)} %refs_4_.1) | copy-start | bytes 6148
  4.2 13.7 %copy-start.3 = (f32[4,9,9,128]{3,0,2,1:T(4,128)S(1)}, f32[4,9,9,128]{3,0,2,1:T(4,128)}, u32[]{:S(2)}) copy-start(f32[4,9,9,128]{3,0,2,1:T(4,128)} %param.21) | copy-start | bytes 497668
  4.3 13.7 %copy-start.5 = (f32[56,9,128]{2,0,1:T(8,128)S(1)}, f32[56,9,128]{2,0,1:T(8,128)}, u32[]{:S(2)}) copy-start(f32[56,9,128]{2,0,1:T(8,128)} %param.14) | copy-start | bytes 774148
  10.3 7.7 %copy-start.1 = (f32[3,9,9,128]{3,0,2,1:T(4,128)S(1)}, f32[3,9,9,128]{3,0,2,1:T(4,128)}, u32[]{:S(2)}) copy-start(f32[3,9,9,128]{3,0,2,1:T(4,128)} %param.15) | copy-start | bytes 373252
  10.3 9.0 %collective-permute-start = (f32[216,128]{1,0:T(8,128)S(1)}, f32[216,128]{1,0:T(8,128)S(1)}, u32[]{:S(2)}, u32[]{:S(2)}) collective-permute-start(f32[216,128]{1,0:T(8,128)S(1)} %get-tuple-element.59), channel_id=1, source_target_pairs={{0,16},{1,17},{2,18},{3,19},{4,20},{5,21},{6,22},{7,23},{8,24},{9,... | collective-permute-start | bytes 331784 | tf_op jit(solution)/shard_map/ppermute | solution.py:420
  13.4 6.0 %collective-permute-start.1 = (f32[216,128]{1,0:T(8,128)S(1)}, f32[216,128]{1,0:T(8,128)S(1)}, u32[]{:S(2)}, u32[]{:S(2)}) collective-permute-start(f32[216,128]{1,0:T(8,128)S(1)} %get-tuple-element.60), channel_id=1, source_target_pairs={{0,4},{1,5},{2,6},{3,7},{4,0},{5,1},{6,2},{7,3},{8,12},{9,13},{10,... | collective-permute-start | bytes 331784 | tf_op jit(solution)/shard_map/ppermute | solution.py:420
  15.0 4.4 %collective-permute-start.2 = (f32[216,128]{1,0:T(8,128)S(1)}, f32[216,128]{1,0:T(8,128)S(1)}, u32[]{:S(2)}, u32[]{:S(2)}) collective-permute-start(f32[216,128]{1,0:T(8,128)S(1)} %get-tuple-element.61), channel_id=1, source_target_pairs={{0,1},{1,0},{2,3},{3,2},{4,8},{5,9},{6,10},{7,11},{8,4},{9,5},{10,... | collective-permute-start | bytes 331784 | tf_op jit(solution)/shard_map/ppermute | solution.py:420
  15.0 4.4 %collective-permute-start.3 = (f32[216,128]{1,0:T(8,128)S(1)}, f32[216,128]{1,0:T(8,128)S(1)}, u32[]{:S(2)}, u32[]{:S(2)}) collective-permute-start(f32[216,128]{1,0:T(8,128)S(1)} %get-tuple-element.62), channel_id=1, source_target_pairs={{0,1},{1,0},{2,3},{3,2},{4,5},{5,4},{6,7},{7,6},{8,9},{9,8},{10,11... | collective-permute-start | bytes 331784 | tf_op jit(solution)/shard_map/ppermute | solution.py:420
  15.5 4.7 %collective-permute-start.4 = (f32[216,128]{1,0:T(8,128)S(1)}, f32[216,128]{1,0:T(8,128)S(1)}, u32[]{:S(2)}, u32[]{:S(2)}) collective-permute-start(f32[216,128]{1,0:T(8,128)S(1)} %get-tuple-element.63), channel_id=1, source_target_pairs={{0,16},{1,2},{2,1},{3,19},{4,20},{5,6},{6,5},{7,23},{8,24},{9,10},... | collective-permute-start | bytes 331784 | tf_op jit(solution)/shard_map/ppermute | solution.py:420
  16.0 0.8 %copy-start.10 = (f32[3,21,21]{2,1,0:T(8,128)S(1)}, f32[3,21,21]{2,1,0:T(8,128)}, u32[]{:S(2)}) copy-start(f32[3,21,21]{2,1,0:T(8,128)} %refs_2_.3) | copy-start | bytes 15880
  18.0 2.2 %copy-start.2 = (f32[4,9,9,128]{3,0,2,1:T(4,128)S(1)}, f32[4,9,9,128]{3,0,2,1:T(4,128)}, u32[]{:S(2)}) copy-start(f32[4,9,9,128]{3,0,2,1:T(4,128)} %param.22) | copy-start | bytes 497668
  26.8 6.5 %collective-permute-start.5 = (f32[216,128]{1,0:T(8,128)S(1)}, f32[216,128]{1,0:T(8,128)S(1)}, u32[]{:S(2)}, u32[]{:S(2)}) collective-permute-start(f32[216,128]{1,0:T(8,128)S(1)} %get-tuple-element.78), channel_id=1, source_target_pairs={{0,16},{1,17},{2,18},{3,19},{4,20},{5,21},{6,22},{7,23},{8,24},{9,... | collective-permute-start | bytes 331784 | tf_op jit(solution)/shard_map/ppermute | solution.py:420
  27.6 5.8 %collective-permute-start.6 = (f32[216,128]{1,0:T(8,128)S(1)}, f32[216,128]{1,0:T(8,128)S(1)}, u32[]{:S(2)}, u32[]{:S(2)}) collective-permute-start(f32[216,128]{1,0:T(8,128)S(1)} %get-tuple-element.79), channel_id=1, source_target_pairs={{0,4},{1,5},{2,6},{3,7},{4,0},{5,1},{6,2},{7,3},{8,12},{9,13},{10,... | collective-permute-start | bytes 331784 | tf_op jit(solution)/shard_map/ppermute | solution.py:420
  30.2 3.2 %collective-permute-start.7 = (f32[216,128]{1,0:T(8,128)S(1)}, f32[216,128]{1,0:T(8,128)S(1)}, u32[]{:S(2)}, u32[]{:S(2)}) collective-permute-start(f32[216,128]{1,0:T(8,128)S(1)} %get-tuple-element.80), channel_id=1, source_target_pairs={{0,1},{1,0},{2,3},{3,2},{4,8},{5,9},{6,10},{7,11},{8,4},{9,5},{10,... | collective-permute-start | bytes 331784 | tf_op jit(solution)/shard_map/ppermute | solution.py:420
  30.2 3.2 %collective-permute-start.8 = (f32[216,128]{1,0:T(8,128)S(1)}, f32[216,128]{1,0:T(8,128)S(1)}, u32[]{:S(2)}, u32[]{:S(2)}) collective-permute-start(f32[216,128]{1,0:T(8,128)S(1)} %get-tuple-element.81), channel_id=1, source_target_pairs={{0,1},{1,0},{2,3},{3,2},{4,5},{5,4},{6,7},{7,6},{8,9},{9,8},{10,11... | collective-permute-start | bytes 331784 | tf_op jit(solution)/shard_map/ppermute | solution.py:420
  30.7 4.7 %collective-permute-start.9 = (f32[216,128]{1,0:T(8,128)S(1)}, f32[216,128]{1,0:T(8,128)S(1)}, u32[]{:S(2)}, u32[]{:S(2)}) collective-permute-start(f32[216,128]{1,0:T(8,128)S(1)} %get-tuple-element.82), channel_id=1, source_target_pairs={{0,16},{1,2},{2,1},{3,19},{4,20},{5,6},{6,5},{7,23},{8,24},{9,10},... | collective-permute-start | bytes 331784 | tf_op jit(solution)/shard_map/ppermute | solution.py:420
  42.2 4.8 %collective-permute-start.10 = (f32[216,128]{1,0:T(8,128)S(1)}, f32[216,128]{1,0:T(8,128)S(1)}, u32[]{:S(2)}, u32[]{:S(2)}) collective-permute-start(f32[216,128]{1,0:T(8,128)S(1)} %get-tuple-element.90), channel_id=1, source_target_pairs={{0,16},{1,17},{2,18},{3,19},{4,20},{5,21},{6,22},{7,23},{8,24},{9,... | collective-permute-start | bytes 331784 | tf_op jit(solution)/shard_map/ppermute | solution.py:420
  43.6 4.7 %collective-permute-start.11 = (f32[216,128]{1,0:T(8,128)S(1)}, f32[216,128]{1,0:T(8,128)S(1)}, u32[]{:S(2)}, u32[]{:S(2)}) collective-permute-start(f32[216,128]{1,0:T(8,128)S(1)} %get-tuple-element.91), channel_id=1, source_target_pairs={{0,4},{1,5},{2,6},{3,7},{4,0},{5,1},{6,2},{7,3},{8,12},{9,13},{10,... | collective-permute-start | bytes 331784 | tf_op jit(solution)/shard_map/ppermute | solution.py:420
  44.1 4.3 %collective-permute-start.12 = (f32[216,128]{1,0:T(8,128)S(1)}, f32[216,128]{1,0:T(8,128)S(1)}, u32[]{:S(2)}, u32[]{:S(2)}) collective-permute-start(f32[216,128]{1,0:T(8,128)S(1)} %get-tuple-element.92), channel_id=1, source_target_pairs={{0,1},{1,0},{2,3},{3,2},{4,8},{5,9},{6,10},{7,11},{8,4},{9,5},{10,... | collective-permute-start | bytes 331784 | tf_op jit(solution)/shard_map/ppermute | solution.py:420
  44.1 4.3 %collective-permute-start.13 = (f32[216,128]{1,0:T(8,128)S(1)}, f32[216,128]{1,0:T(8,128)S(1)}, u32[]{:S(2)}, u32[]{:S(2)}) collective-permute-start(f32[216,128]{1,0:T(8,128)S(1)} %get-tuple-element.93), channel_id=1, source_target_pairs={{0,1},{1,0},{2,3},{3,2},{4,5},{5,4},{6,7},{7,6},{8,9},{9,8},{10,11... | collective-permute-start | bytes 331784 | tf_op jit(solution)/shard_map/ppermute | solution.py:420
  44.6 4.7 %collective-permute-start.14 = (f32[216,128]{1,0:T(8,128)S(1)}, f32[216,128]{1,0:T(8,128)S(1)}, u32[]{:S(2)}, u32[]{:S(2)}) collective-permute-start(f32[216,128]{1,0:T(8,128)S(1)} %get-tuple-element.94), channel_id=1, source_target_pairs={{0,16},{1,2},{2,1},{3,19},{4,20},{5,6},{6,5},{7,23},{8,24},{9,10},... | collective-permute-start | bytes 331784 | tf_op jit(solution)/shard_map/ppermute | solution.py:420
  56.3 4.9 %collective-permute-start.15 = (f32[216,128]{1,0:T(8,128)S(1)}, f32[216,128]{1,0:T(8,128)S(1)}, u32[]{:S(2)}, u32[]{:S(2)}) collective-permute-start(f32[216,128]{1,0:T(8,128)S(1)} %get-tuple-element.102), channel_id=1, source_target_pairs={{0,16},{1,17},{2,18},{3,19},{4,20},{5,21},{6,22},{7,23},{8,24},{9,... | collective-permute-start | bytes 331784 | tf_op jit(solution)/shard_map/ppermute | solution.py:420
  57.0 4.7 %collective-permute-start.16 = (f32[216,128]{1,0:T(8,128)S(1)}, f32[216,128]{1,0:T(8,128)S(1)}, u32[]{:S(2)}, u32[]{:S(2)}) collective-permute-start(f32[216,128]{1,0:T(8,128)S(1)} %get-tuple-element.103), channel_id=1, source_target_pairs={{0,4},{1,5},{2,6},{3,7},{4,0},{5,1},{6,2},{7,3},{8,12},{9,13},{10,... | collective-permute-start | bytes 331784 | tf_op jit(solution)/shard_map/ppermute | solution.py:420
  58.1 3.7 %collective-permute-start.17 = (f32[216,128]{1,0:T(8,128)S(1)}, f32[216,128]{1,0:T(8,128)S(1)}, u32[]{:S(2)}, u32[]{:S(2)}) collective-permute-start(f32[216,128]{1,0:T(8,128)S(1)} %get-tuple-element.104), channel_id=1, source_target_pairs={{0,1},{1,0},{2,3},{3,2},{4,8},{5,9},{6,10},{7,11},{8,4},{9,5},{10,... | collective-permute-start | bytes 331784 | tf_op jit(solution)/shard_map/ppermute | solution.py:420
  58.1 3.7 %collective-permute-start.18 = (f32[216,128]{1,0:T(8,128)S(1)}, f32[216,128]{1,0:T(8,128)S(1)}, u32[]{:S(2)}, u32[]{:S(2)}) collective-permute-start(f32[216,128]{1,0:T(8,128)S(1)} %get-tuple-element.105), channel_id=1, source_target_pairs={{0,1},{1,0},{2,3},{3,2},{4,5},{5,4},{6,7},{7,6},{8,9},{9,8},{10,11... | collective-permute-start | bytes 331784 | tf_op jit(solution)/shard_map/ppermute | solution.py:420
  58.6 4.7 %collective-permute-start.19 = (f32[216,128]{1,0:T(8,128)S(1)}, f32[216,128]{1,0:T(8,128)S(1)}, u32[]{:S(2)}, u32[]{:S(2)}) collective-permute-start(f32[216,128]{1,0:T(8,128)S(1)} %get-tuple-element.106), channel_id=1, source_target_pairs={{0,16},{1,2},{2,1},{3,19},{4,20},{5,6},{6,5},{7,23},{8,24},{9,10},... | collective-permute-start | bytes 331784 | tf_op jit(solution)/shard_map/ppermute | solution.py:420

commit v2 on v1

--- a/solution.py
+++ b/solution.py
@@ -134,9 +134,24 @@
 def put_halves(target, width, row, column, value):
     high, low = halves(value)
     rows, columns = value.shape
-    target[row : row + rows, column : column + columns] = high
-    target[width + row : width + row + rows, column : column + columns] = low
-    target[2 * width + row : 2 * width + row + rows, column : column + columns] = high
+    for part, piece in enumerate((high, low, high)):
+        start = part * width + row
+        if not isinstance(row, int):
+            start = pl.multiple_of(start, 16)
+        target[pl.ds(start, rows), pl.ds(column, columns)] = piece
+
+
+def by_groups(z, group):
+    whole = z.basis // 16
+    group(0, 16)
+
+    def later(index, carry):
+        group(pl.multiple_of(index * 16, 16), 16)
+        return carry
+
+    lax.fori_loop(1, whole, later, 0)
+    if z.basis % 16:
+        group(whole * 16, z.basis % 16)
 
 
 def contract(z, mixed, jacobians, first, rows):
@@ -144,7 +159,7 @@
     for q in range(z.quantities):
         for d in range(3):
             start = d * z.basis + first
-            value = mixed[start : start + rows, q * z.elements : (q + 1) * z.elements]
+            value = mixed[pl.ds(start, rows), q * z.elements : (q + 1) * z.elements]
             for p in range(z.quantities):
                 term = value * jacobians[q, p, d : d + 1, :]
                 totals[p] = term if totals[p] is None else totals[p] + term
@@ -171,11 +186,14 @@
     def derivative(power, carry):
         mixed[...] = product(stiff[...], rhs[...])
         weight = weights[power]
-        for first, rows in z.groups():
+
+        def group(first, rows):
             sums = contract(z, mixed, jacobians, first, rows)
             for p in range(z.quantities):
-                total[p, first : first + rows, :] += sums[p] * weight[0:1, :]
+                total[p, pl.ds(first, rows), :] += sums[p] * weight[0:1, :]
                 put_halves(rhs, z.padded, first, p * e, full_rows(sums[p], 16))
+
+        by_groups(z, group)
         return carry
 
     lax.fori_loop(1, DERIVATIVES, derivative, 0)
@@ -198,14 +216,15 @@
 
 def first_kernel(z, *refs):
     count = len(z.plan)
-    outgoing = refs[7 : 7 + count]
-    table, faces, moments, stiff, project, send_hot = refs[7 + count : 13 + count]
-    rhs, mixed, total, weights, wide_stiff, wide_project = refs[13 + count : 19 + count]
-    held, arrived = refs[19 + count : 26 + count], refs[26 + count]
-    copies = [pltpu.make_async_copy(refs[n], held[n], arrived.at[n]) for n in range(7)]
-    for n in (5, 6, 2, 3, 4, 0, 1):
+    outgoing = refs[8 : 8 + count]
+    table, faces, moments, stiff, project, send_hot, cluster, turns = refs[8 + count : 16 + count]
+    rhs, mixed, total, weights, wide_stiff, wide_project = refs[16 + count : 22 + count]
+    *held, arrived = refs[22 + count :]
+    held = [*held[:4], cluster, *held[4:], turns]
+    copies = [pltpu.make_async_copy(refs[n], held[n], arrived.at[n]) for n in range(8)]
+    for n in (5, 6, 2, 3, 4, 0, 1, 7):
         copies[n].start()
-    solution, jacobians, stiffness, projection, cluster, send_faces, counts = held
+    solution, jacobians, stiffness, projection, _, send_faces, counts, _ = held
     b = z.basis
     for n in (5, 6):
         copies[n].wait()
@@ -220,7 +239,7 @@
     project[...] = left_parts(
         wide_project, [(j * z.face_rows, 0, projection[:, j, :]) for j in range(z.faces)], z.padded
     )
-    for n in (0, 1):
+    for n in (0, 1, 7):
         copies[n].wait()
     predict(
         z, 0, cluster, lambda q, k, n: solution[q, k : k + n, :], jacobians, stiff, project, send_hot,
@@ -230,8 +249,8 @@
 
 def tables_kernel(z, *refs):
     volume, lift, rotation, neighbours, orient = refs[:5]
-    volume_left, lift_left, turned_left, picks, own_hot, far_hot = refs[5:11]
-    wide_volume, wide_lift, wide_turned = refs[11:]
+    volume_left, lift_left, turned_left, picks, own_hot, far_hot, last_hot = refs[5:12]
+    wide_volume, wide_lift, wide_turned = refs[12:]
     e, r, f = z.elements, z.face_rows, z.face_basis
     volume_left[...] = left_parts(wide_volume, [(d * z.basis, 0, volume[d]) for d in range(3)], z.padded)
     plain, turned = [], []
@@ -242,7 +261,13 @@
             value = jnp.dot(face, rotation[o], precision=lax.Precision.HIGHEST, preferred_element_type=F32)
             turned.append((0, o * z.lifted + i * r, value))
     lift_left[...] = left_parts(wide_lift, plain, z.lifted)
-    turned_left[...] = left_parts(wide_turned, turned, z.rotations * z.lifted)
+    wide_turned[...] = jnp.zeros_like(wide_turned)
+    for row, column, value in turned:
+        high = value.astype(BF16).astype(F32)
+        columns = slice(column, column + value.shape[1])
+        wide_turned[: z.basis, columns] = high
+        wide_turned[z.basis :, columns] = value - high
+    turned_left[...] = wide_turned[...].astype(BF16)
     for o in range(z.rotations):
         rows = [
             jnp.broadcast_to(jnp.where(orient[i : i + 1, :] == o, 1.0, 0.0), (r, e)) for i in range(z.faces)
@@ -254,74 +279,98 @@
         for t, entry in enumerate(z.plan):
             _, direction, exists = lists_of(entry)
             offset = jnp.where(exists, z.face_total + direction * z.slots, -z.slots)
-            far_hot[t * z.slots : (t + 1) * z.slots, i * e : (i + 1) * e] = one_hot((z.slots, e), wanted, offset)
+            hot = one_hot((z.slots, e), wanted, offset)
+            if t == len(z.plan) - 1:
+                last_hot[:, i * e : (i + 1) * e] = hot
+            else:
+                far_hot[t * z.slots : (t + 1) * z.slots, i * e : (i + 1) * e] = hot
+
+
+def solve(z, block, solver, store):
+    chunk = 3 if z.quantities % 3 == 0 else 1
+    together = 2 if z.faces % 2 == 0 else 1
+
+    def some(index, carry):
+        for i in range(0, z.faces, together):
+            sums = [[None] * together for _ in range(chunk)]
+            for q in range(z.quantities):
+                for j in range(together):
+                    value = block(q, i + j)
+                    for c in range(chunk):
+                        term = value * solver[q, index * chunk + c, i + j : i + j + 1, :]
+                        sums[c][j] = term if sums[c][j] is None else sums[c][j] + term
+            for c in range(chunk):
+                column = pl.multiple_of((index * chunk + c) * z.elements, z.elements)
+                store(i, together, column, sums[c])
+        return carry
+
+    lax.fori_loop(0, z.quantities // chunk, some, 0)
 
 
 def inner_kernel(z, running, table, faces, moments, jacobians, local_solver, volume_left, lift_left, own_hot, gathered, partial, mixed, rhs):
     e, r = z.elements, z.face_rows
     picked = product(table[...], own_hot[...])
     gathered[...] = picked[: z.block, :] + picked[z.block_padded : z.block_padded + z.block, :]
-    for i in range(z.faces):
-        sums = [None] * z.quantities
-        for q in range(z.quantities):
-            value = faces[i * r : (i + 1) * r, q * e : (q + 1) * e]
-            for p in range(z.quantities):
-                term = value * local_solver[q, p, i : i + 1, :]
-                sums[p] = term if sums[p] is None else sums[p] + term
-        for p in range(z.quantities):
-            partial_rows = slice(i * r, (i + 1) * r)
-            mixed[partial_rows, p * e : (p + 1) * e] = sums[p]
-    put_halves(rhs, z.lifted, 0, 0, mixed[: z.lifted, :])
+    def store(i, j, p, values):
+        put_halves(rhs, z.lifted, i * r, p, jnp.concatenate(values, axis=0))
+
+    solve(z, lambda q, i: faces[i * r : (i + 1) * r, q * e : (q + 1) * e], local_solver, store)
     lifted = product(lift_left[...], rhs[...])
     for q in range(z.quantities):
         partial[q] = running[q] - lifted[:, q * e : (q + 1) * e]
     mixed[...] = product(volume_left[...], moments[...])
-    for first, rows in z.groups():
+
+    def group(first, rows):
         sums = contract(z, mixed, jacobians, first, rows)
         for p in range(z.quantities):
-            partial[p, first : first + rows, :] += sums[p]
+            partial[p, pl.ds(first, rows), :] += sums[p]
+
+    by_groups(z, group)
+
+
+def received_blocks(z, incoming, gathered, far_hot, received):
+    b, half = z.block, z.block_padded
+    for t, source in enumerate(incoming):
+        high, low = halves(full_rows(source[...], half))
+        received[:half, t * z.slots : (t + 1) * z.slots] = high
+        received[half:, t * z.slots : (t + 1) * z.slots] = low
+    picked = product(received[...], far_hot[...])
+    return gathered[...] + picked[:b, :] + picked[half : half + b, :]
+
+
+def early_kernel(z, *refs):
+    *incoming, gathered, far_hot, blocks, received = refs
+    blocks[...] = received_blocks(z, incoming, gathered, far_hot, received)
 
 
 def neighbour_flux(z, incoming, gathered, neighbour_solver, picks, far_hot, turned_left, received, blocks, turned):
-    e, r, b = z.elements, z.face_rows, z.block
-    for t, source in enumerate(incoming):
-        high, low = halves(full_rows(source[...], z.block_padded))
-        received[: z.block_padded, t * z.slots : (t + 1) * z.slots] = high
-        received[z.block_padded :, t * z.slots : (t + 1) * z.slots] = low
-    picked = product(received[...], far_hot[...])
-    blocks[...] = gathered[...] + picked[:b, :] + picked[z.block_padded : z.block_padded + b, :]
+    e, r = z.elements, z.face_rows
+    blocks[...] = received_blocks(z, [incoming], gathered, far_hot, received)
     width = z.rotations * z.lifted
-    for i in range(0, z.faces, 2):
-        per_face = []
-        for j in (i, i + 1):
-            sums = [None] * z.quantities
-            for q in range(z.quantities):
-                value = blocks[q * r : (q + 1) * r, j * e : (j + 1) * e]
-                for p in range(z.quantities):
-                    term = value * neighbour_solver[q, p, j : j + 1, :]
-                    sums[p] = term if sums[p] is None else sums[p] + term
-            per_face.append(sums)
-        for p in range(z.quantities):
-            high, low = halves(jnp.concatenate([per_face[0][p], per_face[1][p]], axis=0))
-            for o in range(z.rotations):
-                pick = picks[o, i * r : (i + 2) * r, :]
-                row = o * z.lifted + i * r
-                chosen = high * pick
-                turned[row : row + 2 * r, p * e : (p + 1) * e] = chosen
-                turned[2 * width + row : 2 * width + row + 2 * r, p * e : (p + 1) * e] = chosen
-                turned[width + row : width + row + 2 * r, p * e : (p + 1) * e] = low * pick
-    return product(turned_left[...], turned[...])
+
+    def store(i, together, column, values):
+        high, low = halves(jnp.concatenate(values, axis=0))
+        rows = together * r
+        for o in range(z.rotations):
+            pick = picks[o, i * r : i * r + rows, :]
+            row = o * z.lifted + i * r
+            turned[row : row + rows, pl.ds(column, e)] = high * pick
+            turned[width + row : width + row + rows, pl.ds(column, e)] = low * pick
+
+    solve(z, lambda q, i: blocks[q * r : (q + 1) * r, i * e : (i + 1) * e], neighbour_solver, store)
+    both = product(turned_left[...], turned[:width, :])
+    return both[: z.basis, :] + both[z.basis :, :] + product(turned_left[: z.basis, :], turned[width:, :])
 
 
 def outer_kernel(z, substep, *refs):
     count = len(z.plan)
-    incoming = refs[:count]
+    incoming = refs[0]
     (gathered, partial, solution, neighbour_solver, picks, far_hot, turned_left, jacobians, stiff, project, send_hot, cluster) = refs[
-        count : count + 12
+        1:13
     ]
-    outgoing = refs[count + 12 : 2 * count + 12]
-    table, faces, moments, updated, running = refs[2 * count + 12 : 2 * count + 17]
-    rhs, mixed, total, weights, received, blocks, turned = refs[2 * count + 17 :]
+    outgoing = refs[13 : 13 + count]
+    table, faces, moments, updated, running = refs[13 + count : 18 + count]
+    rhs, mixed, total, weights, received, blocks, turned = refs[18 + count :]
     e = z.elements
     flux = neighbour_flux(
         z, incoming, gathered, neighbour_solver, picks, far_hot, turned_left, received, blocks, turned
@@ -338,11 +387,7 @@
 
 
 def last_kernel(z, *refs):
-    count = len(z.plan)
-    incoming = refs[:count]
-    gathered, partial, neighbour_solver, picks, far_hot, turned_left = refs[count : count + 6]
-    advanced = refs[count + 6]
-    received, blocks, turned = refs[count + 7 :]
+    incoming, gathered, partial, neighbour_solver, picks, far_hot, turned_left, advanced, received, blocks, turned = refs
     e = z.elements
     flux = neighbour_flux(
         z, incoming, gathered, neighbour_solver, picks, far_hot, turned_left, received, blocks, turned
@@ -402,15 +447,17 @@
     field = ((z.quantities, z.basis, z.elements), F32)
     gathered = ((z.block, z.face_total), F32)
     send_hot = ((z.face_total, count * z.slots), BF16)
-    far_hot = ((count * z.slots, z.face_total), BF16)
+    far_hot = (((count - 1) * z.slots, z.face_total), BF16)
+    last_hot = ((z.slots, z.face_total), BF16)
     own_hot = ((z.face_total, z.face_total), BF16)
     lift_left = ((z.basis, 3 * z.lifted), BF16)
-    turned_left = ((z.basis, 3 * z.rotations * z.lifted), BF16)
+    turned_left = ((2 * z.basis, z.rotations * z.lifted), BF16)
     picks = ((z.rotations, z.lifted, z.elements), BF16)
     mixed = ((3 * z.basis, z.columns), F32)
     weights = ((DERIVATIVES, 8, z.elements), F32)
-    received = ((2 * z.block_padded, count * z.slots), BF16)
-    turned = ((3 * z.rotations * z.lifted, z.columns), BF16)
+    received = ((2 * z.block_padded, (count - 1) * z.slots), BF16)
+    last_received = ((2 * z.block_padded, z.slots), BF16)
+    turned = ((2 * z.rotations * z.lifted, z.columns), BF16)
 
     def wide(entry):
         return (entry[0], F32)
@@ -420,32 +467,39 @@
             lax.ppermute(value, AXES, partners(sizes, entry)) for value, entry in zip(outgoing, plan)
         ]
 
-    first_arguments = (state, jacobians, derivative_stiffness, projection, cluster, send_faces, counts)
+    first_arguments = tuple(
+        pltpu.with_memory_space_constraint(value, pltpu.HBM)
+        for value in (
+            state, jacobians, derivative_stiffness, projection, cluster, send_faces, counts, face_rotation,
+        )
+    )
     results = call(
         functools.partial(first_kernel, z),
-        [block] * count + [table, faces, moments, stiff, project, send_hot],
+        [block] * count
+        + [table, faces, moments, stiff, project, send_hot]
+        + [(value.shape, value.dtype) for value in (cluster, face_rotation)],
         [moments, mixed, field, weights, wide(stiff), wide(project)],
         10_000_000,
         first_arguments,
         space=pltpu.HBM,
         more=[
-            *(pltpu.VMEM(value.shape, value.dtype) for value in first_arguments[:-1]),
+            *(pltpu.VMEM(value.shape, value.dtype) for value in (*first_arguments[:4], send_faces)),
             pltpu.SMEM(counts.shape, counts.dtype),
             pltpu.SemaphoreType.DMA((len(first_arguments),)),
         ],
     )
     outgoing = results[:count]
-    table_now, faces_now, moments_now, stiff_left, project_left, send_matrix = results[count:]
+    table_now, faces_now, moments_now, stiff_left, project_left, send_matrix, cluster, turns = results[count:]
     running = state
     for substep in range(SUBSTEPS):
         incoming = trade(outgoing)
         if substep == 0:
-            volume_left, lift_plain, lift_turned, orient_picks, own_matrix, far_matrix = call(
+            volume_left, lift_plain, lift_turned, orient_picks, own_matrix, far_matrix, last_matrix = call(
                 functools.partial(tables_kernel, z),
-                [stiff, lift_left, turned_left, picks, own_hot, far_hot],
+                [stiff, lift_left, turned_left, picks, own_hot, far_hot, last_hot],
                 [wide(stiff), wide(lift_left), wide(turned_left)],
                 1_000_000,
-                (volume_stiffness, lift, face_rotation, neighbours, orient),
+                (volume_stiffness, lift, turns, neighbours, orient),
             )
         gathered_now, partial = call(
             functools.partial(inner_kernel, z),
@@ -454,22 +508,29 @@
             10_000_000,
             (running, table_now, faces_now, moments_now, jacobians, local_solver, volume_left, lift_plain, own_matrix),
         )
+        (gathered_now,) = call(
+            functools.partial(early_kernel, z),
+            [gathered],
+            [received],
+            5_000_000,
+            (*incoming[:-1], gathered_now, far_matrix),
+        )
         if substep == SUBSTEPS - 1:
             (advanced,) = call(
                 functools.partial(last_kernel, z),
                 [field],
-                [received, gathered, turned],
+                [last_received, gathered, turned],
                 10_000_000,
-                (*incoming, gathered_now, partial, neighbour_solver, orient_picks, far_matrix, lift_turned),
+                (incoming[-1], gathered_now, partial, neighbour_solver, orient_picks, last_matrix, lift_turned),
             )
             return advanced.transpose(1, 0, 2)
         results = call(
             functools.partial(outer_kernel, z, substep),
             [block] * count + [table, faces, moments, field, field],
-            [moments, mixed, field, weights, received, gathered, turned],
+            [moments, mixed, field, weights, last_received, gathered, turned],
             10_000_000,
             (
-                *incoming, gathered_now, partial, state, neighbour_solver, orient_picks, far_matrix, lift_turned,
+                incoming[-1], gathered_now, partial, state, neighbour_solver, orient_picks, last_matrix, lift_turned,
                 jacobians, stiff_left, project_left, send_matrix, cluster,
             ),
         )

time: 65.9 us -> 60.3 us (0.915)
  local copies, waits for them, and re-layouts: 5.02 us -> 0.04 us
  waiting for transfers between devices: 7.81 us -> 5.34 us
  Pallas kernels: 35 us -> 36.3 us
  starting transfers between devices: 17.5 us -> 18.3 us
    unnamed x32 -> x16, local copies, waits for them, and re-layouts: 5.02 us -> 0.04 us
    ppermute x20, waiting for transfers between devices: 7.81 us -> 5.34 us  [trade(): lax.ppermute(value, AXES, partners(sizes, entry))]
    pallas_call x10 -> x14, Pallas kernels: 35 us -> 36.3 us  [call(): pl.pallas_call(body, out_shape=[jax.ShapeDtypeStruct(shape, kind) for sha...]
    ppermute x20, starting transfers between devices: 17.5 us -> 18.3 us  [trade(): lax.ppermute(value, AXES, partners(sizes, entry))]
  transfers between devices with their start and end apart: 20 -> 20, of which waited for: 7 -> 5; matrix products, arithmetic and copies ran while one was open for 0% -> 0% of each run, Pallas kernels for 10% -> 16%
where the time goes in v2:
time: 60.3 us; the launch traced here: 60.2 us
  Pallas kernels  36.3 us (60%)
  starting transfers between devices  18.3 us (30%)
  waiting for transfers between devices  5.34 us (9%)
    pallas_call x14, Pallas kernels, call(): pl.pallas_call(body, out_shape=[jax.ShapeDtypeStruct(shape, kind) for sha...  36.3 us
    ppermute x20, starting transfers between devices, trade(): lax.ppermute(value, AXES, partners(sizes, entry))  18.3 us
    ppermute x20, waiting for transfers between devices, trade(): lax.ppermute(value, AXES, partners(sizes, entry))  5.34 us
  transfers between devices with their start and end apart: 20, of which 5 were waited for; matrix products, arithmetic and copies ran while one was open for 0% of the time, Pallas kernels for 16%

profile of v2, /device:TPU:0, one launch (start us, length us, event | category | flops | bytes accessed | tf_op | source)
XLA Modules:
  0.0 60.2 jit_solution(3575602533280787575)
XLA Ops:
  0.0 0.0 copy-start.3
  0.0 6.0 %shard_map.136 = (f32[216,128]{1,0:T(8,128)S(1)}, f32[216,128]{1,0:T(8,128)S(1)}, f32[216,128]{1,0:T(8,128)S(1)}, f32[216,128]{1,0:T(8,128)S(1)}, f32[216,128]{1...) custom-call(f32[9,56,128]{2,1,0:T(8,128)} %bitcast.25, ...), custom_call_target="tpu_custom_call" | custom-call | flops 10000000 | bytes 1048576 | tf_op jit(solution)/shard_map/pallas_call | solution.py:401
  6.0 0.0 copy-start
  6.0 3.1 %collective-permute-start.1 = (f32[216,128]{1,0:T(8,128)S(1)}, f32[216,128]{1,0:T(8,128)S(1)}, u32[]{:S(2)}, u32[]{:S(2)}) collective-permute-start(f32[216,128]{1,0:T(8,128)S(1)} %get-tuple-element.63), channel_id=1, source_target_pairs={{0,16},{1,17},{2,18},{3,19},{4,20},{5,21},{6,22},{7,23},{8,24},{9,... | collective-permute-start | bytes 331784 | tf_op jit(solution)/shard_map/ppermute | solution.py:467
  9.1 1.6 %collective-permute-start.2 = (f32[216,128]{1,0:T(8,128)S(1)}, f32[216,128]{1,0:T(8,128)S(1)}, u32[]{:S(2)}, u32[]{:S(2)}) collective-permute-start(f32[216,128]{1,0:T(8,128)S(1)} %get-tuple-element.64), channel_id=1, source_target_pairs={{0,4},{1,5},{2,6},{3,7},{4,0},{5,1},{6,2},{7,3},{8,12},{9,13},{10,... | collective-permute-start | bytes 331784 | tf_op jit(solution)/shard_map/ppermute | solution.py:467
  10.7 0.0 collective-permute-start.3
  10.7 0.5 collective-permute-start.4
  11.2 0.5 collective-permute-start
  11.7 0.0 copy-done.4
  11.7 0.0 copy-done.5
  11.7 0.0 copy-done.6
  11.7 0.0 copy-done.7
  11.7 1.2 %shard_map.137 = (bf16[168,192]{1,0:T(8,128)(2,1)S(1)}, bf16[56,288]{1,0:T(8,128)(2,1)S(1)}, bf16[112,288]{1,0:T(8,128)(2,1)S(1)}, bf16[3,96,128]{2,1,0:T(8,128)...) custom-call(f32[3,56,56]{2,1,0:T(8,128)S(1)} %copy-done.4, ...), custom_call_target="tpu_custom_call" | custom-call | flops 1000000 | bytes 1048576 | tf_op jit(solution)/shard_map/pallas_call | solution.py:401
  12.9 0.0 copy-done.2
  12.9 0.0 copy-done.3
  12.9 0.0 copy-done
  12.9 1.8 %shard_map.138 = (f32[216,512]{1,0:T(8,128)S(1)}, f32[9,56,128]{2,1,0:T(8,128)S(1)}) custom-call(f32[9,56,128]{2,1,0:T(8,128)S(1)} %bitcast.26, bf16[448,512]{1,0:T(8,128)(2,1)S(1)} %get-tuple-element.67.table, f32[96,1152]{1,0:T(8,128)S(1)} %get-tuple-element.68.faces, bf16[192,1152]{1,0:T(8,128)(2,1)S(1)} %get-tuple-element.69.moments, ...), custom_call_target="tpu_custom_call" | custom-call | flops 10000000 | bytes 1048576 | tf_op jit(solution)/shard_map/pallas_call | solution.py:401
  14.7 0.0 collective-permute-done.1.refs_0_
  14.7 0.0 collective-permute-done.2.refs_1_
  14.7 0.0 collective-permute-done.3.refs_2_
  14.7 0.0 collective-permute-done.4.refs_3_
  14.7 0.0 copy-start.1
  14.8 0.4 shard_map.139.refs_1_
  15.2 0.8 %collective-permute-done.refs_0_ = f32[216,128]{1,0:T(8,128)S(1)} collective-permute-done((f32[216,128]{1,0:T(8,128)S(1)}, f32[216,128]{1,0:T(8,128)S(1)}, u32[]{:S(2)}, u32[]{:S(2)}) %collective-permute-start) | collective-permute-done | bytes 110624 | tf_op jit(solution)/shard_map/ppermute | solution.py:467
  16.0 6.0 %shard_map.140 = (f32[216,128]{1,0:T(8,128)S(1)}, f32[216,128]{1,0:T(8,128)S(1)}, f32[216,128]{1,0:T(8,128)S(1)}, f32[216,128]{1,0:T(8,128)S(1)}, f32[216,128]{1...) custom-call(f32[216,128]{1,0:T(8,128)S(1)} %collective-permute-done., ...), custom_call_target="tpu_custom_call" | custom-call | flops 10000000 | bytes 1048576 | tf_op jit(solution)/shard_map/pallas_call | solution.py:401
  22.0 1.3 %collective-permute-start.6 = (f32[216,128]{1,0:T(8,128)S(1)}, f32[216,128]{1,0:T(8,128)S(1)}, u32[]{:S(2)}, u32[]{:S(2)}) collective-permute-start(f32[216,128]{1,0:T(8,128)S(1)} %get-tuple-element.85), channel_id=1, source_target_pairs={{0,16},{1,17},{2,18},{3,19},{4,20},{5,21},{6,22},{7,23},{8,24},{9,... | collective-permute-start | bytes 331784 | tf_op jit(solution)/shard_map/ppermute | solution.py:467
  23.3 2.6 %collective-permute-start.7 = (f32[216,128]{1,0:T(8,128)S(1)}, f32[216,128]{1,0:T(8,128)S(1)}, u32[]{:S(2)}, u32[]{:S(2)}) collective-permute-start(f32[216,128]{1,0:T(8,128)S(1)} %get-tuple-element.86), channel_id=1, source_target_pairs={{0,4},{1,5},{2,6},{3,7},{4,0},{5,1},{6,2},{7,3},{8,12},{9,13},{10,... | collective-permute-start | bytes 331784 | tf_op jit(solution)/shard_map/ppermute | solution.py:467
  25.9 0.0 collective-permute-start.8
  25.9 0.5 collective-permute-start.9
  26.4 0.8 %collective-permute-start.5 = (f32[216,128]{1,0:T(8,128)S(1)}, f32[216,128]{1,0:T(8,128)S(1)}, u32[]{:S(2)}, u32[]{:S(2)}) collective-permute-start(f32[216,128]{1,0:T(8,128)S(1)} %get-tuple-element.84), channel_id=1, source_target_pairs={{0,16},{1,2},{2,1},{3,19},{4,20},{5,6},{6,5},{7,23},{8,24},{9,10},... | collective-permute-start | bytes 331784 | tf_op jit(solution)/shard_map/ppermute | solution.py:467
  27.2 1.7 %shard_map.141 = (f32[216,512]{1,0:T(8,128)S(1)}, f32[9,56,128]{2,1,0:T(8,128)S(1)}) custom-call(f32[9,56,128]{2,1,0:T(8,128)S(1)} %get-tuple-element.89.running, bf16[448,512]{1,0:T(8,128)(2,1)S(1)} %get-tuple-element.90.table, f32[96,1152]{1,0:T(8,128)S(1)} %get-tuple-element.91.faces, bf16[192,1152]{1,0:T(8,128)(2,1)S(1)} %get-tuple-element.92.moments, ...), custom_call_target="tpu_custom_call" | custom-call | flops 10000000 | bytes 1048576 | tf_op jit(solution)/shard_map/pallas_call | solution.py:401
  29.0 0.0 collective-permute-done.6.refs_0_
  29.0 0.0 collective-permute-done.7.refs_1_
  29.0 0.0 collective-permute-done.8.refs_2_
  29.0 0.0 collective-permute-done.9.refs_3_
  29.0 0.4 shard_map.142.refs_1_
  29.4 1.7 %collective-permute-done.5.refs_0_ = f32[216,128]{1,0:T(8,128)S(1)} collective-permute-done((f32[216,128]{1,0:T(8,128)S(1)}, f32[216,128]{1,0:T(8,128)S(1)}, u32[]{:S(2)}, u32[]{:S(2)}) %collective-permute-start.5) | collective-permute-done | bytes 110624 | tf_op jit(solution)/shard_map/ppermute | solution.py:467
  31.2 6.0 %shard_map.143 = (f32[216,128]{1,0:T(8,128)S(1)}, f32[216,128]{1,0:T(8,128)S(1)}, f32[216,128]{1,0:T(8,128)S(1)}, f32[216,128]{1,0:T(8,128)S(1)}, f32[216,128]{1...) custom-call(f32[216,128]{1,0:T(8,128)S(1)} %collective-permute-done., ...), custom_call_target="tpu_custom_call" | custom-call | flops 10000000 | bytes 1048576 | tf_op jit(solution)/shard_map/pallas_call | solution.py:401
  37.2 0.9 %collective-permute-start.11 = (f32[216,128]{1,0:T(8,128)S(1)}, f32[216,128]{1,0:T(8,128)S(1)}, u32[]{:S(2)}, u32[]{:S(2)}) collective-permute-start(f32[216,128]{1,0:T(8,128)S(1)} %get-tuple-element.97), channel_id=1, source_target_pairs={{0,16},{1,17},{2,18},{3,19},{4,20},{5,21},{6,22},{7,23},{8,24},{9,... | collective-permute-start | bytes 331784 | tf_op jit(solution)/shard_map/ppermute | solution.py:467
  38.0 0.7 %collective-permute-start.12 = (f32[216,128]{1,0:T(8,128)S(1)}, f32[216,128]{1,0:T(8,128)S(1)}, u32[]{:S(2)}, u32[]{:S(2)}) collective-permute-start(f32[216,128]{1,0:T(8,128)S(1)} %get-tuple-element.98), channel_id=1, source_target_pairs={{0,4},{1,5},{2,6},{3,7},{4,0},{5,1},{6,2},{7,3},{8,12},{9,13},{10,... | collective-permute-start | bytes 331784 | tf_op jit(solution)/shard_map/ppermute | solution.py:467
  38.7 0.0 collective-permute-start.13
  38.7 0.5 collective-permute-start.14
  39.2 1.0 %collective-permute-start.10 = (f32[216,128]{1,0:T(8,128)S(1)}, f32[216,128]{1,0:T(8,128)S(1)}, u32[]{:S(2)}, u32[]{:S(2)}) collective-permute-start(f32[216,128]{1,0:T(8,128)S(1)} %get-tuple-element.96), channel_id=1, source_target_pairs={{0,16},{1,2},{2,1},{3,19},{4,20},{5,6},{6,5},{7,23},{8,24},{9,10},... | collective-permute-start | bytes 331784 | tf_op jit(solution)/shard_map/ppermute | solution.py:467
  40.2 1.7 %shard_map.144 = (f32[216,512]{1,0:T(8,128)S(1)}, f32[9,56,128]{2,1,0:T(8,128)S(1)}) custom-call(f32[9,56,128]{2,1,0:T(8,128)S(1)} %get-tuple-element.101.running, bf16[448,512]{1,0:T(8,128)(2,1)S(1)} %get-tuple-element.102.table, f32[96,1152]{1,0:T(8,128)S(1)} %get-tuple-element.103.faces, bf16[192,1152]{1,0:T(8,128)(2,1)S(1)} %get-tuple-element.104.moments, ...), custom_call_target="tpu_custom_call" | custom-call | flops 10000000 | bytes 1048576 | tf_op jit(solution)/shard_map/pallas_call | solution.py:401
  42.0 0.0 collective-permute-done.11.refs_0_
  42.0 0.8 %collective-permute-done.12.refs_1_ = f32[216,128]{1,0:T(8,128)S(1)} collective-permute-done((f32[216,128]{1,0:T(8,128)S(1)}, f32[216,128]{1,0:T(8,128)S(1)}, u32[]{:S(2)}, u32[]{:S(2)}) %collective-permute-start.12) | collective-permute-done | bytes 110624 | tf_op jit(solution)/shard_map/ppermute | solution.py:467
  42.8 0.0 collective-permute-done.13.refs_2_
  42.8 0.0 collective-permute-done.14.refs_3_
  42.8 0.4 shard_map.145.refs_1_
  43.2 0.8 %collective-permute-done.10.refs_0_ = f32[216,128]{1,0:T(8,128)S(1)} collective-permute-done((f32[216,128]{1,0:T(8,128)S(1)}, f32[216,128]{1,0:T(8,128)S(1)}, u32[]{:S(2)}, u32[]{:S(2)}) %collective-permute-start.10) | collective-permute-done | bytes 110624 | tf_op jit(solution)/shard_map/ppermute | solution.py:467
  44.0 6.5 %shard_map.146 = (f32[216,128]{1,0:T(8,128)S(1)}, f32[216,128]{1,0:T(8,128)S(1)}, f32[216,128]{1,0:T(8,128)S(1)}, f32[216,128]{1,0:T(8,128)S(1)}, f32[216,128]{1...) custom-call(f32[216,128]{1,0:T(8,128)S(1)} %collective-permute-done., ...), custom_call_target="tpu_custom_call" | custom-call | flops 10000000 | bytes 1048576 | tf_op jit(solution)/shard_map/pallas_call | solution.py:401
  50.5 1.0 %collective-permute-start.16 = (f32[216,128]{1,0:T(8,128)S(1)}, f32[216,128]{1,0:T(8,128)S(1)}, u32[]{:S(2)}, u32[]{:S(2)}) collective-permute-start(f32[216,128]{1,0:T(8,128)S(1)} %get-tuple-element.109), channel_id=1, source_target_pairs={{0,16},{1,17},{2,18},{3,19},{4,20},{5,21},{6,22},{7,23},{8,24},{9,... | collective-permute-start | bytes 331784 | tf_op jit(solution)/shard_map/ppermute | solution.py:467
  51.5 1.5 %collective-permute-start.17 = (f32[216,128]{1,0:T(8,128)S(1)}, f32[216,128]{1,0:T(8,128)S(1)}, u32[]{:S(2)}, u32[]{:S(2)}) collective-permute-start(f32[216,128]{1,0:T(8,128)S(1)} %get-tuple-element.110), channel_id=1, source_target_pairs={{0,4},{1,5},{2,6},{3,7},{4,0},{5,1},{6,2},{7,3},{8,12},{9,13},{10,... | collective-permute-start | bytes 331784 | tf_op jit(solution)/shard_map/ppermute | solution.py:467
  53.0 0.0 collective-permute-start.18
  53.0 0.5 collective-permute-start.19
  53.5 1.3 %collective-permute-start.15 = (f32[216,128]{1,0:T(8,128)S(1)}, f32[216,128]{1,0:T(8,128)S(1)}, u32[]{:S(2)}, u32[]{:S(2)}) collective-permute-start(f32[216,128]{1,0:T(8,128)S(1)} %get-tuple-element.108), channel_id=1, source_target_pairs={{0,16},{1,2},{2,1},{3,19},{4,20},{5,6},{6,5},{7,23},{8,24},{9,10},... | collective-permute-start | bytes 331784 | tf_op jit(solution)/shard_map/ppermute | solution.py:467
  54.8 1.7 %shard_map.147 = (f32[216,512]{1,0:T(8,128)S(1)}, f32[9,56,128]{2,1,0:T(8,128)S(1)}) custom-call(f32[9,56,128]{2,1,0:T(8,128)S(1)} %get-tuple-element.113.running, bf16[448,512]{1,0:T(8,128)(2,1)S(1)} %get-tuple-element.114.table, f32[96,1152]{1,0:T(8,128)S(1)} %get-tuple-element.115.faces, bf16[192,1152]{1,0:T(8,128)(2,1)S(1)} %get-tuple-element.116.moments, ...), custom_call_target="tpu_custom_call" | custom-call | flops 10000000 | bytes 1048576 | tf_op jit(solution)/shard_map/pallas_call | solution.py:401
  56.6 0.0 collective-permute-done.16.refs_0_
  56.6 0.0 collective-permute-done.17.refs_1_
  56.6 0.0 collective-permute-done.18.refs_2_
  56.6 0.0 collective-permute-done.19.refs_3_
  56.6 0.4 shard_map.148.refs_1_
  57.0 1.2 %collective-permute-done.15.refs_0_ = f32[216,128]{1,0:T(8,128)S(1)} collective-permute-done((f32[216,128]{1,0:T(8,128)S(1)}, f32[216,128]{1,0:T(8,128)S(1)}, u32[]{:S(2)}, u32[]{:S(2)}) %collective-permute-start.15) | collective-permute-done | bytes 110624 | tf_op jit(solution)/shard_map/ppermute | solution.py:467
  58.3 1.9 %shard_map.149 = f32[9,56,128]{2,1,0:T(8,128)} custom-call(f32[216,128]{1,0:T(8,128)S(1)} %collective-permute-done.15.refs_0_, f32[216,512]{1,0:T(8,128)S(1)} %shard_map.148.refs_1_, f32[9,56,128]{2,1,0:T(8,128)S(1)} %get-tuple-element.118.refs_2_, f32[9,9,4,128]{3,2,1,0:T(4,128)S(1)} %bitcast.20, bf16[3,96,128]{2,1,0:T(8,128)(2,1)S(1)} %get-tuple-element.77.refs_5_.refs_4_, ...), custom_call_target="tpu_custom_call" | custom-call | flops 10000000 | bytes 1048576 | tf_op jit(solution)/shard_map/pallas_call | solution.py:401
  (6 shorter events, 0.0 us)
Async XLA Ops:
  0.0 11.7 %copy-start.4 = (f32[3,56,56]{2,1,0:T(8,128)S(1)}, f32[3,56,56]{2,1,0:T(8,128)}, u32[]{:S(2)}) copy-start(f32[3,56,56]{2,1,0:T(8,128)} %refs_0_.1) | copy-start | bytes 112900
  0.0 11.7 %copy-start.5 = (f32[4,56,21]{1,0,2:T(4,128)S(1)}, f32[4,56,21]{1,0,2:T(4,128)}, u32[]{:S(2)}) copy-start(f32[4,56,21]{1,0,2:T(4,128)} %param.19) | copy-start | bytes 56452
  0.0 11.7 %copy-start.6 = (s32[4,128]{1,0:T(4,128)S(1)}, s32[4,128]{1,0:T(4,128)}, u32[]{:S(2)}) copy-start(s32[4,128]{1,0:T(4,128)} %refs_3_.1) | copy-start | bytes 6148
  0.0 11.7 %copy-start.7 = (s32[4,128]{1,0:T(4,128)S(1)}, s32[4,128]{1,0:T(4,128)}, u32[]{:S(2)}) copy-start(s32[4,128]{1,0:T(4,128)} %refs_4_.1) | copy-start | bytes 6148
  0.0 12.9 %copy-start.2 = (f32[4,9,9,128]{3,0,2,1:T(4,128)S(1)}, f32[4,9,9,128]{3,0,2,1:T(4,128)}, u32[]{:S(2)}) copy-start(f32[4,9,9,128]{3,0,2,1:T(4,128)} %param.21) | copy-start | bytes 497668
  0.0 12.9 %copy-start.3 = (f32[56,9,128]{2,0,1:T(8,128)S(1)}, f32[56,9,128]{2,0,1:T(8,128)}, u32[]{:S(2)}) copy-start(f32[56,9,128]{2,0,1:T(8,128)} %param.14) | copy-start | bytes 774148
  6.0 6.9 %copy-start = (f32[3,9,9,128]{3,0,2,1:T(4,128)S(1)}, f32[3,9,9,128]{3,0,2,1:T(4,128)}, u32[]{:S(2)}) copy-start(f32[3,9,9,128]{3,0,2,1:T(4,128)} %param.15) | copy-start | bytes 373252
  6.0 8.7 %collective-permute-start.1 = (f32[216,128]{1,0:T(8,128)S(1)}, f32[216,128]{1,0:T(8,128)S(1)}, u32[]{:S(2)}, u32[]{:S(2)}) collective-permute-start(f32[216,128]{1,0:T(8,128)S(1)} %get-tuple-element.63), channel_id=1, source_target_pairs={{0,16},{1,17},{2,18},{3,19},{4,20},{5,21},{6,22},{7,23},{8,24},{9,... | collective-permute-start | bytes 331784 | tf_op jit(solution)/shard_map/ppermute | solution.py:467
  9.1 5.6 %collective-permute-start.2 = (f32[216,128]{1,0:T(8,128)S(1)}, f32[216,128]{1,0:T(8,128)S(1)}, u32[]{:S(2)}, u32[]{:S(2)}) collective-permute-start(f32[216,128]{1,0:T(8,128)S(1)} %get-tuple-element.64), channel_id=1, source_target_pairs={{0,4},{1,5},{2,6},{3,7},{4,0},{5,1},{6,2},{7,3},{8,12},{9,13},{10,... | collective-permute-start | bytes 331784 | tf_op jit(solution)/shard_map/ppermute | solution.py:467
  10.7 4.0 %collective-permute-start.3 = (f32[216,128]{1,0:T(8,128)S(1)}, f32[216,128]{1,0:T(8,128)S(1)}, u32[]{:S(2)}, u32[]{:S(2)}) collective-permute-start(f32[216,128]{1,0:T(8,128)S(1)} %get-tuple-element.65), channel_id=1, source_target_pairs={{0,1},{1,0},{2,3},{3,2},{4,8},{5,9},{6,10},{7,11},{8,4},{9,5},{10,... | collective-permute-start | bytes 331784 | tf_op jit(solution)/shard_map/ppermute | solution.py:467
  10.7 4.0 %collective-permute-start.4 = (f32[216,128]{1,0:T(8,128)S(1)}, f32[216,128]{1,0:T(8,128)S(1)}, u32[]{:S(2)}, u32[]{:S(2)}) collective-permute-start(f32[216,128]{1,0:T(8,128)S(1)} %get-tuple-element.66), channel_id=1, source_target_pairs={{0,1},{1,0},{2,3},{3,2},{4,5},{5,4},{6,7},{7,6},{8,9},{9,8},{10,11... | collective-permute-start | bytes 331784 | tf_op jit(solution)/shard_map/ppermute | solution.py:467
  11.2 4.7 %collective-permute-start = (f32[216,128]{1,0:T(8,128)S(1)}, f32[216,128]{1,0:T(8,128)S(1)}, u32[]{:S(2)}, u32[]{:S(2)}) collective-permute-start(f32[216,128]{1,0:T(8,128)S(1)} %get-tuple-element.62), channel_id=1, source_target_pairs={{0,16},{1,2},{2,1},{3,19},{4,20},{5,6},{6,5},{7,23},{8,24},{9,10},... | collective-permute-start | bytes 331784 | tf_op jit(solution)/shard_map/ppermute | solution.py:467
  14.7 1.2 %copy-start.1 = (f32[4,9,9,128]{3,0,2,1:T(4,128)S(1)}, f32[4,9,9,128]{3,0,2,1:T(4,128)}, u32[]{:S(2)}) copy-start(f32[4,9,9,128]{3,0,2,1:T(4,128)} %param.22) | copy-start | bytes 497668
  22.0 7.0 %collective-permute-start.6 = (f32[216,128]{1,0:T(8,128)S(1)}, f32[216,128]{1,0:T(8,128)S(1)}, u32[]{:S(2)}, u32[]{:S(2)}) collective-permute-start(f32[216,128]{1,0:T(8,128)S(1)} %get-tuple-element.85), channel_id=1, source_target_pairs={{0,16},{1,17},{2,18},{3,19},{4,20},{5,21},{6,22},{7,23},{8,24},{9,... | collective-permute-start | bytes 331784 | tf_op jit(solution)/shard_map/ppermute | solution.py:467
  23.3 5.7 %collective-permute-start.7 = (f32[216,128]{1,0:T(8,128)S(1)}, f32[216,128]{1,0:T(8,128)S(1)}, u32[]{:S(2)}, u32[]{:S(2)}) collective-permute-start(f32[216,128]{1,0:T(8,128)S(1)} %get-tuple-element.86), channel_id=1, source_target_pairs={{0,4},{1,5},{2,6},{3,7},{4,0},{5,1},{6,2},{7,3},{8,12},{9,13},{10,... | collective-permute-start | bytes 331784 | tf_op jit(solution)/shard_map/ppermute | solution.py:467
  25.9 3.1 %collective-permute-start.8 = (f32[216,128]{1,0:T(8,128)S(1)}, f32[216,128]{1,0:T(8,128)S(1)}, u32[]{:S(2)}, u32[]{:S(2)}) collective-permute-start(f32[216,128]{1,0:T(8,128)S(1)} %get-tuple-element.87), channel_id=1, source_target_pairs={{0,1},{1,0},{2,3},{3,2},{4,8},{5,9},{6,10},{7,11},{8,4},{9,5},{10,... | collective-permute-start | bytes 331784 | tf_op jit(solution)/shard_map/ppermute | solution.py:467
  25.9 3.1 %collective-permute-start.9 = (f32[216,128]{1,0:T(8,128)S(1)}, f32[216,128]{1,0:T(8,128)S(1)}, u32[]{:S(2)}, u32[]{:S(2)}) collective-permute-start(f32[216,128]{1,0:T(8,128)S(1)} %get-tuple-element.88), channel_id=1, source_target_pairs={{0,1},{1,0},{2,3},{3,2},{4,5},{5,4},{6,7},{7,6},{8,9},{9,8},{10,11... | collective-permute-start | bytes 331784 | tf_op jit(solution)/shard_map/ppermute | solution.py:467
  26.4 4.7 %collective-permute-start.5 = (f32[216,128]{1,0:T(8,128)S(1)}, f32[216,128]{1,0:T(8,128)S(1)}, u32[]{:S(2)}, u32[]{:S(2)}) collective-permute-start(f32[216,128]{1,0:T(8,128)S(1)} %get-tuple-element.84), channel_id=1, source_target_pairs={{0,16},{1,2},{2,1},{3,19},{4,20},{5,6},{6,5},{7,23},{8,24},{9,10},... | collective-permute-start | bytes 331784 | tf_op jit(solution)/shard_map/ppermute | solution.py:467
  37.2 4.8 %collective-permute-start.11 = (f32[216,128]{1,0:T(8,128)S(1)}, f32[216,128]{1,0:T(8,128)S(1)}, u32[]{:S(2)}, u32[]{:S(2)}) collective-permute-start(f32[216,128]{1,0:T(8,128)S(1)} %get-tuple-element.97), channel_id=1, source_target_pairs={{0,16},{1,17},{2,18},{3,19},{4,20},{5,21},{6,22},{7,23},{8,24},{9,... | collective-permute-start | bytes 331784 | tf_op jit(solution)/shard_map/ppermute | solution.py:467
  38.0 4.7 %collective-permute-start.12 = (f32[216,128]{1,0:T(8,128)S(1)}, f32[216,128]{1,0:T(8,128)S(1)}, u32[]{:S(2)}, u32[]{:S(2)}) collective-permute-start(f32[216,128]{1,0:T(8,128)S(1)} %get-tuple-element.98), channel_id=1, source_target_pairs={{0,4},{1,5},{2,6},{3,7},{4,0},{5,1},{6,2},{7,3},{8,12},{9,13},{10,... | collective-permute-start | bytes 331784 | tf_op jit(solution)/shard_map/ppermute | solution.py:467
  38.7 4.1 %collective-permute-start.13 = (f32[216,128]{1,0:T(8,128)S(1)}, f32[216,128]{1,0:T(8,128)S(1)}, u32[]{:S(2)}, u32[]{:S(2)}) collective-permute-start(f32[216,128]{1,0:T(8,128)S(1)} %get-tuple-element.99), channel_id=1, source_target_pairs={{0,1},{1,0},{2,3},{3,2},{4,8},{5,9},{6,10},{7,11},{8,4},{9,5},{10,... | collective-permute-start | bytes 331784 | tf_op jit(solution)/shard_map/ppermute | solution.py:467
  38.7 4.1 %collective-permute-start.14 = (f32[216,128]{1,0:T(8,128)S(1)}, f32[216,128]{1,0:T(8,128)S(1)}, u32[]{:S(2)}, u32[]{:S(2)}) collective-permute-start(f32[216,128]{1,0:T(8,128)S(1)} %get-tuple-element.100), channel_id=1, source_target_pairs={{0,1},{1,0},{2,3},{3,2},{4,5},{5,4},{6,7},{7,6},{8,9},{9,8},{10,11... | collective-permute-start | bytes 331784 | tf_op jit(solution)/shard_map/ppermute | solution.py:467
  39.2 4.7 %collective-permute-start.10 = (f32[216,128]{1,0:T(8,128)S(1)}, f32[216,128]{1,0:T(8,128)S(1)}, u32[]{:S(2)}, u32[]{:S(2)}) collective-permute-start(f32[216,128]{1,0:T(8,128)S(1)} %get-tuple-element.96), channel_id=1, source_target_pairs={{0,16},{1,2},{2,1},{3,19},{4,20},{5,6},{6,5},{7,23},{8,24},{9,10},... | collective-permute-start | bytes 331784 | tf_op jit(solution)/shard_map/ppermute | solution.py:467
  50.5 6.1 %collective-permute-start.16 = (f32[216,128]{1,0:T(8,128)S(1)}, f32[216,128]{1,0:T(8,128)S(1)}, u32[]{:S(2)}, u32[]{:S(2)}) collective-permute-start(f32[216,128]{1,0:T(8,128)S(1)} %get-tuple-element.109), channel_id=1, source_target_pairs={{0,16},{1,17},{2,18},{3,19},{4,20},{5,21},{6,22},{7,23},{8,24},{9,... | collective-permute-start | bytes 331784 | tf_op jit(solution)/shard_map/ppermute | solution.py:467
  51.5 5.0 %collective-permute-start.17 = (f32[216,128]{1,0:T(8,128)S(1)}, f32[216,128]{1,0:T(8,128)S(1)}, u32[]{:S(2)}, u32[]{:S(2)}) collective-permute-start(f32[216,128]{1,0:T(8,128)S(1)} %get-tuple-element.110), channel_id=1, source_target_pairs={{0,4},{1,5},{2,6},{3,7},{4,0},{5,1},{6,2},{7,3},{8,12},{9,13},{10,... | collective-permute-start | bytes 331784 | tf_op jit(solution)/shard_map/ppermute | solution.py:467
  53.0 3.6 %collective-permute-start.18 = (f32[216,128]{1,0:T(8,128)S(1)}, f32[216,128]{1,0:T(8,128)S(1)}, u32[]{:S(2)}, u32[]{:S(2)}) collective-permute-start(f32[216,128]{1,0:T(8,128)S(1)} %get-tuple-element.111), channel_id=1, source_target_pairs={{0,1},{1,0},{2,3},{3,2},{4,8},{5,9},{6,10},{7,11},{8,4},{9,5},{10,... | collective-permute-start | bytes 331784 | tf_op jit(solution)/shard_map/ppermute | solution.py:467
  53.0 3.6 %collective-permute-start.19 = (f32[216,128]{1,0:T(8,128)S(1)}, f32[216,128]{1,0:T(8,128)S(1)}, u32[]{:S(2)}, u32[]{:S(2)}) collective-permute-start(f32[216,128]{1,0:T(8,128)S(1)} %get-tuple-element.112), channel_id=1, source_target_pairs={{0,1},{1,0},{2,3},{3,2},{4,5},{5,4},{6,7},{7,6},{8,9},{9,8},{10,11... | collective-permute-start | bytes 331784 | tf_op jit(solution)/shard_map/ppermute | solution.py:467
  53.5 4.7 %collective-permute-start.15 = (f32[216,128]{1,0:T(8,128)S(1)}, f32[216,128]{1,0:T(8,128)S(1)}, u32[]{:S(2)}, u32[]{:S(2)}) collective-permute-start(f32[216,128]{1,0:T(8,128)S(1)} %get-tuple-element.108), channel_id=1, source_target_pairs={{0,16},{1,2},{2,1},{3,19},{4,20},{5,6},{6,5},{7,23},{8,24},{9,10},... | collective-permute-start | bytes 331784 | tf_op jit(solution)/shard_map/ppermute | solution.py:467
